TPU v7x, 32 devices: a whole 2x2x4 slice. The times are simulated.
32 devices in a mesh: group: 4 (over x, core), tensor: 8 (over z, y).
Axes of the slice: x: 2, y: 2, z: 4, core: 2. Of those that a mesh axis runs over, the one named last changes fastest.
Arguments:
- hidden: bfloat16 [512, 8192], P('group'), may hold values from -6 to 6
- norm_gain: bfloat16 [8192], replicated, may hold values from 0.5 to 1.5
- query_matrix: bfloat16 [8192, 8192], P(None, 'tensor'), may hold values from -0.0625 to 0.0625
- output_weight: bfloat16 [8192, 8192], P('tensor'), may hold values from -0.0625 to 0.0625
- kv_pages: bfloat16 [768, 8, 32, 256], P('group', 'tensor'), may hold values from -400 to 400
- page_order: int32 [4, 192], P('group'), may hold values from 0 to 191, each once within a row
- page_counts: int32 [4, 128], P('group'), may hold values from 1 to 8, 192 in all within a row
- page_trims: int32 [4, 128], P('group'), may hold values from 0 to 31
- adapter_store: bfloat16 [32, 8192, 256], P('group', 'tensor'), may hold values from -0.0625 to 0.0625
- store_route: int32 [32, 1], replicated, may hold values from 0 to 3; in each aligned block of 8 rows (0 to 7, 8 to 15, ...) at most 4 rows name the same one
- store_slot: int32 [32], replicated, may hold values from 0 to 7
Outputs:
- layer_out: bfloat16 [512, 8192], P('group')
Inputs may be any that keep to these rules, and one draw needn't show every extreme that they name: `store_route`: in each group's block of 8 segments no store group is named more than 4 times. `page_order`: each group's row names each of its 192 pages once. `page_counts`: each group's counts sum to 192.
All inputs are finite; a program needn't handle non-finite values.
Results may differ from a plain program's by a relative error of at most 0.0092.
Values may be sent and summed in bfloat16 or wider, within the bound.
No kernel may reach another device: no remote copies, remote signals or barrier semaphores. Data moves between devices by JAX's collectives and lax.ppermute only.
A program may use at most 128 MiB of HBM per device.

v0:
```python
import math

import jax
import jax.numpy as jnp
from jax import lax
from jax.sharding import PartitionSpec as P

KVH = 8
HD = 128
SEG = 16
PAGES_MAX = 8


adapter_scale = 2.0
norm_eps = 1e-05
rope_base = 500000.0


def partner_2(value, axis, stride):
    return lax.ppermute(value, axis, [(i, i ^ 1 << stride) for i in range(lax.axis_size(axis))])


def rotate(queries, positions):
    half_dim = queries.shape[-1] // 2
    frequency = rope_base ** (-(jnp.arange(half_dim).astype(jnp.float32) * 2.0) / queries.shape[-1])
    angles = positions[:, None] * frequency[None, :]
    cosine = jnp.cos(angles)[:, None, :]
    sine_table = jnp.sin(angles)[:, None, :]
    lower_part = queries[..., :half_dim]
    upper_part = queries[..., half_dim:]
    return jnp.concatenate(
        [
            lower_part * cosine - upper_part * sine_table,
            upper_part * cosine + lower_part * sine_table,
        ],
        axis=-1,
    )


def rank_total(partial_value):
    return lax.psum(partial_value, "tensor")


def body(
    hidden,
    norm_gain,
    query_matrix,
    output_weight,
    kv_pages,
    page_order,
    page_counts,
    page_trims,
    adapter_store,
    store_route,
    store_slot,
):
    tensor_size = lax.axis_size("tensor")
    group_size = lax.axis_size("group")
    shard_tensor_index = lax.axis_index("tensor")
    group_index = lax.axis_index("group")
    row_count = hidden.shape[0]
    local_width = query_matrix.shape[1]
    heads_dev = local_width // HD
    split_count = tensor_size // KVH
    part_index = shard_tensor_index % split_count
    pool_size = kv_pages.shape[0]
    half_size = kv_pages.shape[2]
    stored = adapter_store.shape[0]
    lane_count = adapter_store.shape[2]
    adapter_rank_width = lane_count // 4
    seg_count = row_count // SEG
    capacity = max(2, (2 * seg_count + group_size - 1) // group_size)
    hidden_float32 = hidden.astype(jnp.float32)
    inv_rms = lax.rsqrt(jnp.mean(hidden_float32 * hidden_float32, axis=1, keepdims=True) + norm_eps)
    normalized_hidden = (hidden_float32 * inv_rms * norm_gain.astype(jnp.float32)[None, :]).astype(
        jnp.bfloat16
    )
    normalized_local = lax.dynamic_slice_in_dim(
        normalized_hidden, shard_tensor_index * local_width, local_width, 1
    )
    route_table = store_route[:, 0].reshape(group_size, seg_count)
    slot_table = store_slot.reshape(group_size, seg_count)
    earlier = jnp.arange(seg_count)[:, None] > jnp.arange(seg_count)[None, :]
    same_route = route_table[:, :, None] == route_table[:, None, :]
    slot_rank = jnp.sum(jnp.where(same_route & earlier[None, :, :], 1, 0), axis=2).astype(jnp.int32)
    target = route_table * capacity + slot_rank
    own_target = lax.dynamic_index_in_dim(target, group_index, 0, keepdims=False)
    placing = (jnp.arange(group_size * capacity)[:, None] == own_target[None, :]).astype(
        jnp.bfloat16
    )
    wanted = (route_table == group_index)[:, :, None] & (
        slot_rank[:, :, None] == jnp.arange(capacity)[None, None, :]
    )
    slot_hot = slot_table[:, :, None] == jnp.arange(stored)[None, None, :]
    choosing = (
        jnp.einsum("gkc,gka->gca", wanted.astype(jnp.float32), slot_hot.astype(jnp.float32))
        .reshape(group_size * capacity, stored)
        .astype(jnp.bfloat16)
    )
    store_flat = adapter_store.reshape(stored, local_width * lane_count)
    outgoing = jnp.dot(choosing, store_flat, preferred_element_type=jnp.float32).astype(
        jnp.bfloat16
    )
    chosen = outgoing.reshape(group_size * capacity, local_width, lane_count)

    def apply_adapter_update(input_rows, leading_column, trailing_column):
        sending = jnp.dot(
            placing,
            input_rows.reshape(seg_count, SEG * local_width),
            preferred_element_type=jnp.float32,
        ).astype(jnp.bfloat16)
        received = lax.all_to_all(
            sending.reshape(group_size, capacity * SEG, local_width),
            "group",
            split_axis=0,
            concat_axis=0,
            tiled=True,
        )
        received = received.reshape(group_size * capacity, SEG, local_width)
        partial_value = jnp.einsum(
            "nsd,ndr->nsr",
            received,
            chosen[:, :, leading_column : leading_column + adapter_rank_width],
            preferred_element_type=jnp.float32,
        )
        low_rank = rank_total(partial_value).astype(jnp.bfloat16)
        result = jnp.einsum(
            "nsr,ndr->nsd",
            low_rank,
            chosen[:, :, trailing_column : trailing_column + adapter_rank_width],
            preferred_element_type=jnp.float32,
        )
        returned = lax.all_to_all(
            result.reshape(group_size, capacity * SEG, local_width),
            "group",
            split_axis=0,
            concat_axis=0,
            tiled=True,
        )
        returned = returned.reshape(group_size * capacity, SEG * local_width)
        gathered = jnp.dot(
            placing.T.astype(jnp.float32),
            returned,
            precision=lax.Precision.HIGHEST,
            preferred_element_type=jnp.float32,
        )
        return gathered.reshape(row_count, local_width)

    lengths = page_counts[0] * split_count * half_size - page_trims[0]
    query_float32 = jnp.dot(
        normalized_hidden, query_matrix, preferred_element_type=jnp.float32
    ) + adapter_scale * apply_adapter_update(normalized_local, 0, 2 * adapter_rank_width)
    queries = rotate(
        query_float32.reshape(row_count, heads_dev, HD), (lengths - 1).astype(jnp.float32)
    ).astype(jnp.bfloat16)
    for level_bit in range(split_count.bit_length() - 1):
        partner = partner_2(queries, "tensor", level_bit)
        upper_bit = shard_tensor_index // 2**level_bit % 2
        queries = jnp.where(
            upper_bit == 0,
            jnp.concatenate([queries, partner], axis=1),
            jnp.concatenate([partner, queries], axis=1),
        )
    offsets = jnp.cumsum(page_counts[0]) - page_counts[0]
    page_slot = jnp.clip(
        offsets[:, None] + jnp.arange(PAGES_MAX, dtype=jnp.int32)[None, :], 0, pool_size - 1
    )
    page_ids = page_order[0][page_slot]
    cached = kv_pages[:, 0][page_ids].reshape(row_count, PAGES_MAX * half_size, 2 * HD)
    positions = (
        jnp.arange(PAGES_MAX, dtype=jnp.int32)[:, None] * (split_count * half_size)
        + part_index * half_size
        + jnp.arange(half_size, dtype=jnp.int32)[None, :]
    ).reshape(-1)
    usable = positions[None, :] < lengths[:, None]
    scores = jnp.einsum(
        "rgd,rpd->rgp", queries, cached[..., :HD], preferred_element_type=jnp.float32
    ) / math.sqrt(HD)
    masked = jnp.where(usable[:, None, :], scores, -1e30)
    row_max = jnp.max(masked, axis=2)
    weights = jnp.where(usable[:, None, :], jnp.exp(masked - row_max[..., None]), 0.0).astype(
        jnp.bfloat16
    )
    totals = jnp.sum(weights.astype(jnp.float32), axis=2)
    output_part = jnp.einsum(
        "rgp,rpd->rgd", weights, cached[..., HD:], preferred_element_type=jnp.float32
    )
    for level_bit in range(split_count.bit_length() - 1):
        other_out, other_max, other_total = partner_2(
            (output_part, row_max, totals), "tensor", level_bit
        )
        joint_max = jnp.maximum(row_max, other_max)
        own_scale = jnp.exp(row_max - joint_max)
        other_scale = jnp.exp(other_max - joint_max)
        output_part = output_part * own_scale[..., None] + other_out * other_scale[..., None]
        totals = totals * own_scale + other_total * other_scale
        row_max = joint_max
    attended_all = output_part / totals[..., None]
    attention_result = (
        lax.dynamic_slice_in_dim(attended_all, part_index * heads_dev, heads_dev, 1)
        .reshape(row_count, local_width)
        .astype(jnp.bfloat16)
    )
    partial_output = jnp.dot(attention_result, output_weight, preferred_element_type=jnp.float32)
    adapter_output = adapter_scale * apply_adapter_update(
        attention_result, adapter_rank_width, 3 * adapter_rank_width
    )
    own_cols = (
        lax.dynamic_slice_in_dim(partial_output, shard_tensor_index * local_width, local_width, 1)
        + adapter_output
    )
    partial_output = lax.dynamic_update_slice_in_dim(
        partial_output, own_cols, shard_tensor_index * local_width, 1
    )
    summed = lax.psum(partial_output, "tensor")
    layer_out = (hidden_float32 + summed).astype(jnp.bfloat16)
    return layer_out


def solution(mesh):
    in_specs = (
        P("group", None),
        P(),
        P(None, "tensor"),
        P("tensor", None),
        P("group", "tensor", None, None),
        P("group", None),
        P("group", None),
        P("group", None),
        P("group", "tensor", None),
        P(),
        P(),
    )
    out_specs = P("group", None)
    return jax.shard_map(body, mesh=mesh, in_specs=in_specs, out_specs=out_specs, check_vma=False)
```

profile of v0, /device:TPU:0, one launch (start us, length us, event | category | flops | bytes accessed | tf_op | source)
XLA Modules:
  0.0 380.9 jit_solution(1167026221294067381)
XLA Ops:
  6.5 2.2 fusion.5
  11.7 2.2 fusion.7
  20.2 4.2 %all-to-all-start = ((bf16[4,64,1024]{2,1,0:T(8,128)(2,1)}), bf16[4,64,1024]{2,1,0:T(8,128)(2,1)}, u32[]{:S(2)}, u32[]{:S(2)}) async-start(bf16[4,64,1024]{2,1,0:T(8,128)(2,1)} %reshape.285), calls=%async_computation | async-start | bytes 1048576 | tf_op jit(solution)/shard_map/all_to_all | solution.py:112
  25.3 6.8 %gather_fusion = s32[1024]{0:T(1024)S(1)} fusion(s32[192]{0:T(256)S(1)} %bitcast.51, s32[1024]{0:T(1024)S(1)} %broadcast_clamp_fusion), kind=kCustom, calls=%fused_computation | custom fusion | bytes 12288 | tf_op jit(solution)/shard_map/gather | solution.py:168
  32.4 4.6 %copy.27 = bf16[1,8,1024,256]{3,1,2,0:T(8,128)(2,1)S(1)} copy(bf16[1,8,1024,256]{3,2,1,0:T(8,128)(2,1)} %bitcast.61) | data formatting | bytes 8388608
  37.1 5.5 %convolution_convert_fusion = bf16[16,262144]{1,0:T(8,128)(2,1)} fusion(bf16[16,8]{1,0:T(8,128)(2,1)S(1)} %bitcast.65, bf16[8,262144]{1,0:T(8,128)(2,1)S(1)} %bitcast.59), kind=kOutput, calls=%fused_computation.3 | convolution fusion | flops 71303168 | bytes 12583168 | tf_op jit(solution)/shard_map/dot_general | solution.py:101
  42.7 8.5 %copy.28 = bf16[2,8,1024,256]{3,2,1,0:T(8,128)(2,1)} copy(bf16[2,8,1024,256]{3,1,2,0:T(8,128)(2,1)} %bitcast.56) | data formatting | bytes 16777216
  51.1 3.0 fusion.15
  54.2 40.2 %psum.21 = bf16[16,16,64]{2,1,0:T(8,128)(2,1)S(1)} all-reduce(f32[16,16,64]{2,1,0:T(8,128)S(1)} %fusion.15), channel_id=1, replica_groups=mesh['group'=4,'tensor'=8] {'tensor'}, use_global_device_ids=true, to_apply=%region_2.3 | all-reduce | flops 16384 | bytes 98304 | tf_op jit(solution)/shard_map/psum | solution.py:41
  94.4 4.4 %fusion.13 = f32[16,16,1024]{2,1,0:T(8,128)} fusion(bf16[16,1024,256]{2,1,0:T(8,128)(2,1)} %bitcast.53, bf16[16,16,64]{2,1,0:T(8,128)(2,1)S(1)} %psum.21), kind=kOutput, calls=%fused_computation.23 | convolution fusion | flops 33554432 | bytes 5275648 | tf_op jit(solution)/shard_map/nsr,ndr->nsd/dot_general | solution.py:127
  98.7 4.4 %all-to-all-start.1 = ((f32[4,64,1024]{2,1,0:T(8,128)}), f32[4,64,1024]{2,1,0:T(8,128)}, u32[]{:S(2)}, u32[]{:S(2)}) async-start(f32[4,64,1024]{2,1,0:T(8,128)} %bitcast.62), calls=%async_computation.1 | async-start | bytes 2097152 | tf_op jit(solution)/shard_map/all_to_all | solution.py:133
  103.2 12.4 %gather_fusion.1 = bf16[1024,32,256]{2,1,0:T(8,128)(2,1)} fusion(bf16[192,32,256]{2,1,0:T(8,128)(2,1)S(1)} %bitcast.50, s32[1024]{0:T(1024)S(1)} %broadcast_clamp_fusion.1), kind=kCustom, calls=%fused_computation.1 | custom fusion | bytes 33558528 | tf_op jit(solution)/shard_map/gather | solution.py:169
  121.4 8.1 %fusion.27 = f32[16,8,8,128]{3,1,2,0:T(8,128)S(1)} fusion(f32[128,1024]{1,0:T(8,128)S(1)} %mul.135, bf16[128,8192]{1,0:T(8,128)(2,1)S(1)} %copy-done.4, bf16[8192,1024]{1,0:T(8,128)(2,1)} %param.13), kind=kOutput, calls=%fused_computation.34 | convolution fusion | flops 2147614720 | bytes 19922944 | tf_op jit(solution)/shard_map/dot_general | solution.py:150
  129.9 5.9 %convert_reduce_fusion = (f32[128,8]{1,0:T(8,128)S(1)}, bf16[128,8,256]{2,1,0:T(8,128)(2,1)S(1)}) fusion(pred[128,256]{1,0:T(8,128)(4,1)S(1)} %broadcast_compare_fusion, bf16[128,256,256]{2,1,0:T(8,128)(2,1)} %bitcast.57, bf16[128,8,64]{2,1,0:T(8,128)(2,1)S(1)} %get-tuple-element.8, bf16[128,8,64]{2,1,0:T(8,128)(2,1)S(1)} %get-tuple-element.7), kind=kOutput, calls=%fused_computation.36 | convolution fusion | flops 69468416 | bytes 9506816 | tf_op jit(solution)/shard_map/sub | solution.py:181
  135.8 4.6 %fusion.31 = bf16[128,8,128]{2,1,0:T(8,128)(2,1)S(1)} fusion(bf16[128,8,256]{2,1,0:T(8,128)(2,1)S(1)} %get-tuple-element.13, bf16[128,256,256]{2,1,0:T(8,128)(2,1)} %bitcast.58, f32[128,8]{1,0:T(8,128)S(1)} %get-tuple-element.12), kind=kOutput, calls=%fused_computation.38 | convolution fusion | flops 67371008 | bytes 9179136 | tf_op jit(solution)/shard_map/rgp,rpd->rgd/dot_general | solution.py:185
  141.0 11.2 %all_to_all.20 = bf16[4,64,1024]{2,1,0:T(8,128)(2,1)S(1)} all-to-all(bf16[4,64,1024]{2,1,0:T(8,128)(2,1)S(1)} %reshape.295), channel_id=1, replica_groups=mesh['group'=4,'tensor'=8] {'group'}, dimensions={0} | all-to-all | bytes 1048576 | tf_op jit(solution)/shard_map/all_to_all | solution.py:112
  152.2 3.5 fusion.11
  155.7 34.2 %psum.22 = bf16[16,16,64]{2,1,0:T(8,128)(2,1)S(1)} all-reduce(f32[16,16,64]{2,1,0:T(8,128)S(1)} %fusion.11), channel_id=1, replica_groups=mesh['group'=4,'tensor'=8] {'tensor'}, use_global_device_ids=true, to_apply=%region_6.7 | all-reduce | flops 16384 | bytes 98304 | tf_op jit(solution)/shard_map/psum | solution.py:41
  189.9 4.5 %fusion.9 = f32[16,16,1024]{2,1,0:T(8,128)} fusion(bf16[16,1024,256]{2,1,0:T(8,128)(2,1)} %bitcast.55, bf16[16,16,64]{2,1,0:T(8,128)(2,1)S(1)} %psum.22), kind=kOutput, calls=%fused_computation.19 | convolution fusion | flops 33554432 | bytes 5275648 | tf_op jit(solution)/shard_map/nsr,ndr->nsd/dot_general | solution.py:127
  194.3 3.5 all-to-all-start.3
  198.1 10.1 %fusion.34 = f32[128,8192]{1,0:T(8,128)} fusion(bf16[1024,8192]{1,0:T(8,128)(2,1)} %param.14, bf16[16,8,8,128]{3,2,1,0:T(8,128)(2,1)S(1)} %bitcast.64), kind=kOutput, calls=%fused_computation.42 | convolution fusion | flops 2147483648 | bytes 21233664 | tf_op jit(solution)/shard_map/dot_general | solution.py:204
  208.2 4.0 %all-to-all-done.3 = f32[4,64,1024]{2,1,0:T(8,128)S(1)} async-done(((f32[4,64,1024]{2,1,0:T(8,128)}), f32[4,64,1024]{2,1,0:T(8,128)S(1)}, u32[]{:S(2)}, u32[]{:S(2)}) %all-to-all-start.3) | async-done | bytes 1048608 | tf_op jit(solution)/shard_map/all_to_all | solution.py:133
  215.0 154.5 %all-reduce.2.cloned.1.call-done = f32[128,8192]{1,0:T(8,128)} async-done(((f32[128,8192]{1,0:T(8,128)}), f32[128,8192]{1,0:T(8,128)}) %all-reduce.2.cloned.1.call-update) | async-done | bytes 4194320 | tf_op jit(solution)/shard_map/psum | solution.py:215
  369.5 4.6 %fusion.8 = bf16[128,8192]{1,0:T(8,128)(2,1)} fusion(f32[128,8192]{1,0:T(8,128)} %all-reduce.2.cloned.1.call-done, bf16[128,8192]{1,0:T(8,128)(2,1)} %param.11), kind=kLoop, calls=%fused_computation.18 | loop fusion | flops 3145728 | bytes 8388608 | tf_op jit(solution)/shard_map/convert_element_type | solution.py:216
  (65 shorter events, 20.1 us)
Async XLA Ops:
  6.5 96.6 %copy-start = (bf16[192,1,32,256]{3,2,1,0:T(8,128)(2,1)S(1)}, bf16[192,1,32,256]{3,2,1,0:T(8,128)(2,1)}, u32[]{:S(2)}) copy-start(bf16[192,1,32,256]{3,2,1,0:T(8,128)(2,1)} %param.15) | copy-start | bytes 9437188
  8.8 15.7 %copy-start.6 = (s32[32]{0:T(128)S(1)}, s32[32]{0:T(128)}, u32[]{:S(2)}) copy-start(s32[32]{0:T(128)} %param.21) | copy-start | bytes 388
  8.8 15.9 %copy-start.5 = (s32[1,128]{1,0:T(1,128)S(1)}, s32[1,128]{1,0:T(1,128)}, u32[]{:S(2)}) copy-start(s32[1,128]{1,0:T(1,128)} %param.17) | copy-start | bytes 1540
  11.7 13.4 %copy-start.7 = (s32[1,128]{1,0:T(1,128)S(1)}, s32[1,128]{1,0:T(1,128)}, u32[]{:S(2)}) copy-start(s32[1,128]{1,0:T(1,128)} %param.18) | copy-start | bytes 1540
  11.7 13.6 %copy-start.2 = (s32[1,192]{1,0:T(1,128)S(1)}, s32[1,192]{1,0:T(1,128)}, u32[]{:S(2)}) copy-start(s32[1,192]{1,0:T(1,128)} %param.16) | copy-start | bytes 2308
  13.9 1.3 copy-start.3
  20.2 30.9 %all-to-all-start = ((bf16[4,64,1024]{2,1,0:T(8,128)(2,1)}), bf16[4,64,1024]{2,1,0:T(8,128)(2,1)}, u32[]{:S(2)}, u32[]{:S(2)}) async-start(bf16[4,64,1024]{2,1,0:T(8,128)(2,1)} %reshape.285), calls=%async_computation | async-start | bytes 1048576 | tf_op jit(solution)/shard_map/all_to_all | solution.py:112
  98.7 18.7 %all-to-all-start.1 = ((f32[4,64,1024]{2,1,0:T(8,128)}), f32[4,64,1024]{2,1,0:T(8,128)}, u32[]{:S(2)}, u32[]{:S(2)}) async-start(f32[4,64,1024]{2,1,0:T(8,128)} %bitcast.62), calls=%async_computation.1 | async-start | bytes 2097152 | tf_op jit(solution)/shard_map/all_to_all | solution.py:133
  115.6 5.8 %copy-start.4 = (bf16[128,8192]{1,0:T(8,128)(2,1)S(1)}, bf16[128,8192]{1,0:T(8,128)(2,1)}, u32[]{:S(2)}) copy-start(bf16[128,8192]{1,0:T(8,128)(2,1)} %copy-done.3) | copy-start | bytes 6291460
  194.3 17.9 %all-to-all-start.3 = ((f32[4,64,1024]{2,1,0:T(8,128)}), f32[4,64,1024]{2,1,0:T(8,128)S(1)}, u32[]{:S(2)}, u32[]{:S(2)}) async-start(f32[4,64,1024]{2,1,0:T(8,128)} %bitcast.11), calls=%async_computation.3 | async-start | bytes 2097152 | tf_op jit(solution)/shard_map/all_to_all | solution.py:133
  197.9 171.6 %all-reduce.2.cloned.1.call-start = ((), (), s32[]{:S(2)}) async-start(), calls=%async_computation.4 | async-start | bytes 8388608 | tf_op jit(solution)/shard_map/psum | solution.py:215
  215.0 159.1 %copy-start.1 = (bf16[192,1,32,256]{3,2,1,0:T(8,128)(2,1)S(1)}, bf16[192,1,32,256]{3,2,1,0:T(8,128)(2,1)}, u32[]{:S(2)}) copy-start(bf16[192,1,32,256]{3,2,1,0:T(8,128)(2,1)} %param.15) | copy-start | bytes 9437188
Sparse Core Ops, SparseCore 0:
  215.1 154.3 all-reduce.1
where the time goes:
time: 382 us; the launch traced here: 381 us
  waiting for transfers between devices  160 us (42%)
  blocking collectives  85.6 us (22%)
  matrix products  53.8 us (14%)
  local copies, waits for them, and re-layouts  41.1 us (11%)
  other arithmetic  14.4 us (4%)
  between operations  13.7 us (4%)
  starting transfers between devices  12.4 us (3%)
    psum x1, waiting for transfers between devices, body(): summed = lax.psum(partial_output, 'tensor')  154 us
    psum x2, blocking collectives, rank_total(): return lax.psum(partial_value, 'tensor')  74.4 us
    unnamed x20, local copies, waits for them, and re-layouts  15 us
    gather x1, local copies, waits for them, and re-layouts, body(): kv_pages[:, 0][page_ids].reshape(row_count, PAGES_MAX * half_size, 2 * HD)  12.4 us
    all_to_all x1, blocking collectives, apply_adapter_update(): lax.all_to_all(sending.reshape(group_size, capacity * SEG, local_width),...  11.2 us
    dot_general x1, matrix products, body(): jnp.dot(attention_result, output_weight, preferred_element_type=jnp.float32)  10.1 us
    dot_general x2, matrix products, apply_adapter_update(): jnp.einsum('nsr,ndr->nsd', low_rank, chosen[:, :, trailing_column:trailin...  8.83 us
    dot_general x1, matrix products, body(): jnp.dot(normalized_hidden, query_matrix, preferred_element_type=jnp.float32)  8.1 us
  transfers between devices with their start and end apart: 4, of which 3 were waited for; matrix products, arithmetic and copies ran while one was open for 13% of the time, Pallas kernels for 0%

commit v1 on v0

v1 whole, which is shorter than its diff:
```python
import functools
import math

import jax
import jax.numpy as jnp
from jax import lax
from jax.experimental import pallas as pl
from jax.experimental.pallas import tpu as pltpu
from jax.sharding import PartitionSpec as P

KVH = 8
HD = 128
SEG = 16
PAGES_MAX = 8
LANES = 128
SLOTS = 8

adapter_scale = 2.0
norm_eps = 1e-05
rope_base = 500000.0
hidden_mask = -1e30

f32 = jnp.float32
bf16 = jnp.bfloat16
VMEM = pl.BlockSpec(memory_space=pltpu.VMEM)
SMEM = pl.BlockSpec(memory_space=pltpu.SMEM)
NT = (((1,), (1,)), ((), ()))
TN = (((0,), (0,)), ((), ()))


def cost(flops, traffic):
    return pl.CostEstimate(flops=int(flops), bytes_accessed=int(traffic), transcendentals=0)


def params():
    return pltpu.CompilerParams(vmem_limit_bytes=48 << 20)


def flip(value, axis, bits):
    return lax.ppermute(value, axis, [(i, i ^ bits) for i in range(lax.axis_size(axis))])


def tables(positions):
    half = HD // 2
    frequency = rope_base ** (-(jnp.arange(half).astype(f32) * 2.0) / HD)
    angles = positions[:, None] * frequency[None, :]
    cosine, sine = jnp.cos(angles), jnp.sin(angles)
    return jnp.concatenate([cosine, cosine], 1), jnp.concatenate([-sine, sine], 1)


def prep_kernel(half_size, counts_ref, trims_ref, owner_ref, mask_ref, row_ref):
    slots, rows = owner_ref.shape
    counts = counts_ref[...].astype(f32)
    trims = trims_ref[...].astype(f32)
    before = lax.broadcasted_iota(jnp.int32, (rows, rows), 0)
    after = lax.broadcasted_iota(jnp.int32, (rows, rows), 1)
    earlier = jnp.where(before < after, 1.0, 0.0).astype(bf16)
    start = jnp.dot(
        jnp.broadcast_to(counts, (8, rows)).astype(bf16), earlier, preferred_element_type=f32
    )[0:1]
    end = start + counts
    slot = lax.broadcasted_iota(jnp.int32, (slots, rows), 0).astype(f32)
    owner = jnp.where((slot >= start) & (slot < end), 1.0, 0.0)
    owner_ref[...] = owner
    last = jnp.where(slot == end - 1.0, trims, 0.0)
    used = half_size - jnp.sum(last, axis=1, keepdims=True)
    row = lax.broadcasted_iota(jnp.int32, (slots, rows), 1).astype(f32)
    row_ref[...] = jnp.broadcast_to(
        jnp.sum(owner * row, axis=1, keepdims=True), row_ref.shape
    )
    shape = mask_ref.shape
    place = lax.broadcasted_iota(jnp.int32, shape, 0) % SLOTS
    column = lax.broadcasted_iota(jnp.int32, shape, 1)
    fits = (column // half_size == place) & ((column % half_size).astype(f32) < used)
    mask_ref[...] = jnp.where(fits, 0.0, hidden_mask)


def prepare(counts, trims, slots, half_size):
    rows = counts.shape[1]
    return pl.pallas_call(
        functools.partial(prep_kernel, half_size),
        out_shape=(
            jax.ShapeDtypeStruct((slots, rows), f32),
            jax.ShapeDtypeStruct((slots, SLOTS * half_size), f32),
            jax.ShapeDtypeStruct((slots, LANES), f32),
        ),
        in_specs=[VMEM, VMEM],
        out_specs=(VMEM, VMEM, VMEM),
        compiler_params=params(),
        cost_estimate=cost(1e6, 5e5),
        name="prep",
    )(counts, trims)


def attention_kernel(
    heads, extra, fused, order_ref, query_ref, inv_ref, *refs
):
    deltas, refs = refs[:extra], refs[extra:]
    cos_ref, sin_ref, owner_ref, mask_ref, row_ref, kv_ref = refs[:6]
    outs = refs[6:-4]
    q_scr, o_scr, m_scr, l_scr = refs[-4:]
    slots = owner_ref.shape[0]
    steps = slots // SLOTS
    half_size = kv_ref.shape[2]
    owner = owner_ref[...]
    owner_low = owner.astype(bf16)
    for head in range(heads):
        lanes = slice(head * HD, (head + 1) * HD)
        value = query_ref[:, lanes]
        if fused:
            for ref in deltas:
                value = value + adapter_scale * ref[0, :, lanes].astype(f32)
            value = value * inv_ref[...]
            value = value * cos_ref[...] + pltpu.roll(value, HD // 2, 1) * sin_ref[...]
        spread = jnp.dot(owner_low, value.astype(bf16), preferred_element_type=f32)
        q_scr[:, head * SLOTS : (head + 1) * SLOTS, :] = spread.reshape(steps, SLOTS, HD)

    def step(b, carry):
        pages = [kv_ref[order_ref[0, b * SLOTS + i], 0] for i in range(SLOTS)]
        keys = jnp.concatenate([page[:, :HD] for page in pages], axis=0)
        values = jnp.concatenate([page[:, HD:] for page in pages], axis=0)
        scores = lax.dot_general(
            q_scr[b].astype(bf16), keys, NT, preferred_element_type=f32
        ) * (1.0 / math.sqrt(HD))
        width = SLOTS * half_size
        mask = mask_ref[pl.ds(pl.multiple_of(b * SLOTS, SLOTS), SLOTS), :]
        scores = (scores.reshape(heads, SLOTS, width) + mask[None]).reshape(heads * SLOTS, width)
        top = jnp.max(scores, axis=1, keepdims=True)
        weights = jnp.exp(scores - top).astype(bf16)
        total = jnp.sum(weights.astype(f32), axis=1, keepdims=True)
        o_scr[b] = jnp.dot(weights, values, preferred_element_type=f32)
        m_scr[b] = jnp.broadcast_to(top, (heads * SLOTS, LANES))
        l_scr[b] = jnp.broadcast_to(total, (heads * SLOTS, LANES))
        return carry

    lax.fori_loop(0, steps, step, 0, unroll=4 if steps % 4 == 0 else 1)

    lane = lax.broadcasted_iota(jnp.int32, (slots, LANES), 1)
    tops = jnp.zeros((slots, LANES), f32)
    totals = jnp.zeros((slots, LANES), f32)
    for head in range(heads):
        part = slice(head * SLOTS, (head + 1) * SLOTS)
        tops = jnp.where(lane == head, m_scr[:, part, :].reshape(slots, LANES), tops)
        totals = jnp.where(lane == head, l_scr[:, part, :].reshape(slots, LANES), totals)
    row = row_ref[...]
    joint = tops
    distance = 1
    while distance < PAGES_MAX:
        for shift in (distance, slots - distance):
            same = pltpu.roll(row, shift, 0) == row
            joint = jnp.where(same, jnp.maximum(joint, pltpu.roll(joint, shift, 0)), joint)
        distance *= 2
    factor = jnp.exp(tops - joint)
    dot = functools.partial(
        lax.dot_general,
        dimension_numbers=TN,
        precision=lax.Precision.HIGHEST,
        preferred_element_type=f32,
    )
    denom = dot(owner, totals * factor)
    for head in range(heads):
        part = slice(head * SLOTS, (head + 1) * SLOTS)
        lanes = slice(head * HD, (head + 1) * HD)
        value = o_scr[:, part, :].reshape(slots, HD) * factor[:, head : head + 1]
        numer = dot(owner, value)
        if fused:
            outs[0][:, lanes] = (numer / denom[:, head : head + 1]).astype(bf16)
        else:
            outs[0][:, lanes] = numer
    if not fused:
        previous = pltpu.roll(row, 1, 0) == row
        first = jnp.where(previous, 0.0, owner)
        outs[1][...] = dot(first, joint)
        outs[2][...] = denom


def attend(query, inv, deltas, cosine, sine, owner, mask, row, order, pages, fused):
    rows = query.shape[0]
    slots = owner.shape[0]
    heads = query.shape[1] // HD
    width = query.shape[1]
    if fused:
        out_shape = (jax.ShapeDtypeStruct((rows, width), bf16),)
    else:
        small = jax.ShapeDtypeStruct((rows, LANES), f32)
        out_shape = (jax.ShapeDtypeStruct((rows, width), f32), small, small)
    first = pl.BlockSpec((1, rows, width), lambda i: (0, 0, 0))

    def whole(value):
        return pl.BlockSpec(value.shape, lambda i, n=value.ndim: (0,) * n)

    steps = slots // SLOTS
    scratch = pltpu.VMEM((steps, heads * SLOTS, LANES), f32)
    fixed = (cosine, sine, owner, mask, row, pages)
    return pl.pallas_call(
        functools.partial(attention_kernel, heads, len(deltas), fused),
        grid=(1,),
        out_shape=out_shape,
        in_specs=[SMEM, whole(query), whole(inv)]
        + [first] * len(deltas)
        + [whole(value) for value in fixed],
        out_specs=tuple(pl.BlockSpec(s.shape, lambda i: (0, 0)) for s in out_shape),
        scratch_shapes=[scratch] * 4,
        compiler_params=params(),
        cost_estimate=cost(4e8, 8e6),
        name="attend",
    )(order, query, inv, *deltas, *fixed)


def down_kernel(offset, places, stored, aid_ref, *refs):
    inputs, (store_ref, out_ref, y_scr) = refs[: len(places)], refs[len(places) :]
    members = sum(len(group) for group in places)
    rows = inputs[0].shape[1]
    blocks = [None] * members
    for ref, group in zip(inputs, places):
        for i, j in enumerate(group):
            blocks[j] = (ref, i)
    for j in range(members):
        ref, i = blocks[j]
        for a in range(0, stored, 2):
            pair = jnp.concatenate([store_ref[a], store_ref[a + 1]], axis=1)
            result = jnp.dot(ref[i], pair, preferred_element_type=f32)
            y_scr[a, j * rows : (j + 1) * rows, :] = result[:, :LANES]
            y_scr[a + 1, j * rows : (j + 1) * rows, :] = result[:, LANES:]
    half = LANES // 2
    left = lax.broadcasted_iota(jnp.int32, (SEG, LANES), 1) < half
    seg_count = rows // SEG

    def pick(j, k):
        index = aid_ref[j * seg_count + k]
        value = y_scr[jnp.maximum(index, 0), pl.ds(j * rows + k * SEG, SEG), :]
        return jnp.where(index >= 0, value, 0.0)

    for j in range(0, members, 2):
        for k in range(seg_count):
            even, odd = pick(j, k), pick(j + 1, k)
            if offset:
                even = pltpu.roll(even, half, 1)
            else:
                odd = pltpu.roll(odd, half, 1)
            out_ref[pl.ds((j // 2) * rows + k * SEG, SEG), :] = jnp.where(
                left, even, odd
            ).astype(bf16)


def project_down(aid, arrays, store, offset):
    stored, width, _ = store.shape
    rows = arrays[0][0].shape[1]
    members = sum(value.shape[0] for value, _ in arrays)
    return pl.pallas_call(
        functools.partial(down_kernel, offset, [places for _, places in arrays], stored),
        grid=(1,),
        out_shape=jax.ShapeDtypeStruct((members // 2 * rows, LANES), bf16),
        in_specs=[SMEM]
        + [pl.BlockSpec(value.shape, lambda i: (0, 0, 0)) for value, _ in arrays]
        + [pl.BlockSpec((stored, width, LANES), lambda i: (0, 0, 0))],
        out_specs=pl.BlockSpec((members // 2 * rows, LANES), lambda i: (0, 0)),
        scratch_shapes=[pltpu.VMEM((stored, members * rows, LANES), f32)],
        compiler_params=params(),
        cost_estimate=cost(2 * members * rows * width * stored * LANES, 6e6),
        name="down",
    )(aid, *[value for value, _ in arrays], store)


def up_kernel(offset, members, stored, aid_ref, rank_ref, store_ref, keep_ref, send_ref, l_scr):
    rows = keep_ref.shape[1]
    half = LANES // 2
    seg_count = rows // SEG
    left = lax.broadcasted_iota(jnp.int32, (SEG, LANES), 1) < half
    for j in range(members):
        for k in range(seg_count):
            index = aid_ref[j * seg_count + k]
            value = rank_ref[pl.ds((j // 2) * rows + k * SEG, SEG), :].astype(f32)
            if (j % 2 == 1) != offset:
                value = pltpu.roll(value, half, 1)
            value = jnp.where(left != offset, value, 0.0)
            for a in range(stored):
                l_scr[pl.ds(j * rows + k * SEG, SEG), a * LANES : (a + 1) * LANES] = jnp.where(
                    index == a, value, 0.0
                ).astype(bf16)
    factors = jnp.concatenate([store_ref[a] for a in range(stored)], axis=1)
    for j in range(members):
        result = lax.dot_general(
            l_scr[j * rows : (j + 1) * rows, :], factors, NT, preferred_element_type=f32
        ).astype(bf16)
        (send_ref if j % 2 else keep_ref)[j // 2] = result


def project_up(aid, rank, store, members, rows, offset):
    stored, width, _ = store.shape
    half = jax.ShapeDtypeStruct((members // 2, rows, width), bf16)
    spec = pl.BlockSpec(half.shape, lambda i: (0, 0, 0))
    return pl.pallas_call(
        functools.partial(up_kernel, offset, members, stored),
        grid=(1,),
        out_shape=(half, half),
        in_specs=[
            SMEM,
            pl.BlockSpec(rank.shape, lambda i: (0, 0)),
            pl.BlockSpec((stored, width, LANES), lambda i: (0, 0, 1)),
        ],
        out_specs=(spec, spec),
        scratch_shapes=[pltpu.VMEM((members * rows, stored * LANES), bf16)],
        compiler_params=params(),
        cost_estimate=cost(2 * members * rows * width * stored * LANES, 6e6),
        name="up",
    )(aid, rank, store)


def block_dot_kernel(columns_ref, rows_ref, weight_ref, out_ref):
    out_ref[0] = jnp.dot(rows_ref[...], weight_ref[...], preferred_element_type=f32).astype(bf16)


def block_dot(columns, rows, weight, width):
    count = columns.shape[0]
    return pl.pallas_call(
        block_dot_kernel,
        grid_spec=pltpu.PrefetchScalarGridSpec(
            num_scalar_prefetch=1,
            grid=(count,),
            in_specs=[
                pl.BlockSpec(rows.shape, lambda i, table: (0, 0)),
                pl.BlockSpec((weight.shape[0], width), lambda i, table: (0, table[i])),
            ],
            out_specs=pl.BlockSpec((1, rows.shape[0], width), lambda i, table: (i, 0, 0)),
        ),
        out_shape=jax.ShapeDtypeStruct((count, rows.shape[0], width), bf16),
        compiler_params=params(),
        cost_estimate=cost(
            2 * count * rows.size * width, count * width * (weight.shape[0] + rows.shape[0]) * 2
        ),
        name="block_dot",
    )(columns, rows, weight)


def assemble_kernel(layout, columns_ref, *refs):
    inputs, (out_ref, sem) = refs[: len(layout)], refs[len(layout) :]
    copies = []
    for ref, (first, count) in zip(inputs, layout):
        width = ref.shape[2]
        for i in range(count):
            column = pl.multiple_of(columns_ref[first + i], LANES)
            copies.append(
                pltpu.make_async_copy(
                    ref.at[i], out_ref.at[:, pl.ds(column, width)], sem.at[first + i]
                )
            )
    for copy in copies:
        copy.start()
    for copy in copies:
        copy.wait()


def assemble(columns, arrays, full):
    rows = arrays[0].shape[1]
    layout, first = [], 0
    for value in arrays:
        layout.append((first, value.shape[0]))
        first += value.shape[0]
    return pl.pallas_call(
        functools.partial(assemble_kernel, layout),
        out_shape=jax.ShapeDtypeStruct((rows, full), bf16),
        in_specs=[SMEM] + [VMEM] * len(arrays),
        out_specs=pl.BlockSpec(memory_space=pl.ANY),
        scratch_shapes=[pltpu.SemaphoreType.DMA((first,))],
        compiler_params=params(),
        cost_estimate=cost(0, 4 * rows * full),
        name="assemble",
    )(columns, *arrays)


def gather_rows(own, axis, size):
    arrays = [(own[None], [0])]
    for bit in reversed(range(size.bit_length() - 1)):
        arrays = arrays + [
            (flip(value, axis, 1 << bit), [j ^ (1 << bit) for j in places])
            for value, places in arrays
        ]
    return arrays


def return_rows(keep, send, axis, size):
    addends = []
    for bit in range(size.bit_length() - 1):
        received = flip(send, axis, 1 << bit)
        addends = addends + [received] if bit else [keep, received]
        if keep.shape[0] == 1:
            break
        total = functools.reduce(jnp.add, [value.astype(f32) for value in addends]).astype(bf16)
        send = total[1::2]
        addends = [value[0::2] for value in addends]
        keep = addends[0]
    return addends


def body(
    hidden,
    norm_gain,
    query_matrix,
    output_weight,
    kv_pages,
    page_order,
    page_counts,
    page_trims,
    adapter_store,
    store_route,
    store_slot,
):
    tensor_size = lax.axis_size("tensor")
    group_size = lax.axis_size("group")
    tensor_index = lax.axis_index("tensor")
    group_index = lax.axis_index("group")
    rows, model = hidden.shape
    width = query_matrix.shape[1]
    heads_dev = width // HD
    split_count = tensor_size // KVH
    part_index = tensor_index % split_count
    slots = kv_pages.shape[0]
    half_size = kv_pages.shape[2]
    seg_count = rows // SEG

    hidden_wide = hidden.astype(f32)
    gain = norm_gain.astype(f32)
    own_hidden = lax.dynamic_slice_in_dim(hidden, tensor_index * width, width, 1).astype(f32)
    own_gain = lax.dynamic_slice_in_dim(gain, tensor_index * width, width, 0)
    own_rows = (own_hidden * own_gain[None, :]).astype(bf16)
    row_blocks = gather_rows(own_rows, "group", group_size)

    members = jnp.arange(group_size) ^ group_index
    routes = store_route[:, 0].reshape(group_size, seg_count)[members]
    slot_of = store_slot.reshape(group_size, seg_count)[members]
    aid = jnp.where(routes == group_index, slot_of, -1).reshape(-1).astype(jnp.int32)

    inv = lax.rsqrt(jnp.mean(hidden_wide * hidden_wide, axis=1, keepdims=True) + norm_eps)
    scaled = (hidden_wide * gain[None, :]).astype(bf16)
    query = jnp.dot(scaled, query_matrix, preferred_element_type=f32)

    lengths = page_counts[0] * (split_count * half_size) - page_trims[0]
    cosine, sine = tables((lengths - 1).astype(f32))
    trims = page_trims * jnp.where(part_index == split_count - 1, 1, 0)
    owner, mask, row = prepare(page_counts, trims, slots, half_size)

    bits = tensor_size.bit_length() - 1
    steps = [1 << k for k in range(bits - 1)] + [3 << (bits - 2)]

    def adapter(blocks, offset):
        rank = project_down(aid, blocks, adapter_store, offset)
        for step in steps:
            rank = (rank.astype(f32) + flip(rank, "tensor", step).astype(f32)).astype(bf16)
        keep, send = project_up(aid, rank, adapter_store, group_size, rows, offset)
        return return_rows(keep, send, "group", group_size)

    deltas = adapter(row_blocks, False)
    attention = functools.partial(
        attend,
        cosine=cosine,
        sine=sine,
        owner=owner,
        mask=mask,
        row=row,
        order=page_order,
        pages=kv_pages,
    )
    if split_count == 1:
        (attended,) = attention(query, inv, deltas, fused=True)
    else:
        delta = functools.reduce(jnp.add, [value[0].astype(f32) for value in deltas])
        wide = ((query + adapter_scale * delta) * inv).reshape(rows, heads_dev, HD)
        wide = wide * cosine[:, None] + jnp.roll(wide, HD // 2, 2) * sine[:, None]
        queries = wide.astype(bf16)
        levels = split_count.bit_length() - 1
        for level in range(levels):
            partner = flip(queries, "tensor", 1 << level)
            upper = part_index // 2**level % 2
            queries = jnp.where(
                upper == 0,
                jnp.concatenate([queries, partner], axis=1),
                jnp.concatenate([partner, queries], axis=1),
            )
        heads = heads_dev * split_count
        numer, top, total = attention(
            queries.reshape(rows, heads * HD).astype(f32), inv, [], fused=False
        )
        numer = numer.reshape(rows, heads, HD)
        top, total = top[:, :heads], total[:, :heads]
        for level in range(levels):
            other, other_top, other_total = flip((numer, top, total), "tensor", 1 << level)
            joint = jnp.maximum(top, other_top)
            own_scale, other_scale = jnp.exp(top - joint), jnp.exp(other_top - joint)
            numer = numer * own_scale[..., None] + other * other_scale[..., None]
            total = total * own_scale + other_total * other_scale
            top = joint
        attended = (
            lax.dynamic_slice_in_dim(
                numer / total[..., None], part_index * heads_dev, heads_dev, 1
            )
            .reshape(rows, width)
            .astype(bf16)
        )

    part_count = 2
    part_width = width // part_count
    orders = [[(p + i) % bits for i in range(bits)] for p in range(part_count)]

    def relative(order, first):
        found = []
        for n in range(1 << (bits - 1)):
            offset = steps[order[0]] if first else 0
            for i, k in enumerate(order[1:]):
                if n >> (bits - 2 - i) & 1:
                    offset ^= steps[k]
            found.append(offset)
        return found

    def columns_of(offsets, p):
        return ((jnp.array(offsets, jnp.int32) ^ tensor_index) * part_count + p).astype(jnp.int32)

    def partial(p, first):
        return block_dot(
            columns_of(relative(orders[p], first), p), attended, output_weight, part_width
        )

    row_blocks = gather_rows(attended, "group", group_size)
    sends = [partial(p, True) for p in range(part_count)]
    moving = [flip(sends[p], "tensor", steps[orders[p][0]]) for p in range(part_count)]
    keeps = [partial(p, False) for p in range(part_count)]
    deltas = adapter(row_blocks, True)
    own_delta = functools.reduce(jnp.add, [value[0].astype(f32) for value in deltas])
    finished = []
    for p in range(part_count):
        addends = [keeps[p], moving[p]]
        for k in orders[p][1:]:
            half = addends[0].shape[0] // 2
            send = functools.reduce(jnp.add, [v[half:].astype(f32) for v in addends]).astype(bf16)
            addends = [v[:half] for v in addends] + [flip(send, "tensor", steps[k])]
        total = functools.reduce(jnp.add, [v[0].astype(f32) for v in addends])
        lanes = slice(p * part_width, (p + 1) * part_width)
        total = total + own_hidden[:, lanes] + adapter_scale * own_delta[:, lanes]
        finished.append(total.astype(bf16)[None])

    arrays, table = [], []
    for p in range(part_count):
        value, offsets = finished[p], [0]
        for k in reversed(orders[p]):
            received = flip(value, "tensor", steps[k])
            other = [j ^ steps[k] for j in offsets]
            if len(offsets) * 2 == tensor_size:
                arrays += [value, received]
                table += [(j, p) for j in offsets + other]
            else:
                value = jnp.concatenate([value, received], axis=0)
                offsets = offsets + other
    offsets = jnp.array([j for j, _ in table], jnp.int32) ^ tensor_index
    columns = offsets * width + jnp.array([p * part_width for _, p in table], jnp.int32)
    return assemble(columns.astype(jnp.int32), arrays, model)


def solution(mesh):
    in_specs = (
        P("group", None),
        P(),
        P(None, "tensor"),
        P("tensor", None),
        P("group", "tensor", None, None),
        P("group", None),
        P("group", None),
        P("group", None),
        P("group", "tensor", None),
        P(),
        P(),
    )
    out_specs = P("group", None)
    return jax.shard_map(body, mesh=mesh, in_specs=in_specs, out_specs=out_specs, check_vma=False)
```

time: 382 us -> 169 us (0.44)
  waiting for transfers between devices: 160 us -> 65.8 us
  blocking collectives: 85.6 us -> 0 us
  matrix products: 53.8 us -> 8.9 us
  Pallas kernels: 0 us -> 39.1 us
  local copies, waits for them, and re-layouts: 41.1 us -> 9.46 us
  starting transfers between devices: 12.4 us -> 38.2 us
  between operations: 13.7 us -> 0.56 us
  other arithmetic: 14.4 us -> 6.3 us
    psum x1 -> x0, waiting for transfers between devices: 154 us -> none  [body(): summed = lax.psum(partial_output, 'tensor')]
    psum x2 -> x0, blocking collectives: 74.4 us -> none  [rank_total(): return lax.psum(partial_value, 'tensor')]
    ppermute x0 -> x28, waiting for transfers between devices: none -> 65.8 us  [flip(): lax.ppermute(value, axis, [(i, i ^ bits) for i in range(lax.axis_size(axi...]
    pallas_call x0 -> x11, Pallas kernels: none -> 39.1 us  [the longest x4 16.3 us: block_dot(): pl.pallas_call(block_dot_kernel, grid_spec=pltpu.PrefetchScalarGridSpec(n...]
    dot_general x13 -> x1, matrix products: 48 us -> 8.9 us  [body(): query = jnp.dot(scaled, query_matrix, preferred_element_type=f32)]
    ppermute x0 -> x28, starting transfers between devices: none -> 38.2 us  [flip(): lax.ppermute(value, axis, [(i, i ^ bits) for i in range(lax.axis_size(axi...]
    gather x3 -> x2, local copies, waits for them, and re-layouts: 19.4 us -> 1.12 us  [the longest x1 0.56 us: body(): slot_of = store_slot.reshape(group_size, seg_count)[members]]
    all_to_all x3 -> x0, starting transfers between devices: 12.2 us -> none  [the longest x2 7.95 us: apply_adapter_update(): lax.all_to_all(result.reshape(group_size, capacity * SEG, local_width), '...]
  transfers between devices with their start and end apart: 4 -> 28, of which waited for: 3 -> 17; matrix products, arithmetic and copies ran while one was open for 13% -> 10% of each run, Pallas kernels for 0% -> 12%
where the time goes in v1:
time: 169 us; the launch traced here: 168 us
  waiting for transfers between devices  65.8 us (39%)
  Pallas kernels  39.1 us (23%)
  starting transfers between devices  38.2 us (23%)
  local copies, waits for them, and re-layouts  9.46 us (6%)
  matrix products  8.9 us (5%)
  other arithmetic  6.3 us (4%)
    ppermute x28, waiting for transfers between devices, flip(): lax.ppermute(value, axis, [(i, i ^ bits) for i in range(lax.axis_size(axi...  65.8 us
    ppermute x28, starting transfers between devices, flip(): lax.ppermute(value, axis, [(i, i ^ bits) for i in range(lax.axis_size(axi...  38.2 us
    pallas_call x4, Pallas kernels, block_dot(): pl.pallas_call(block_dot_kernel, grid_spec=pltpu.PrefetchScalarGridSpec(n...  16.3 us
    pallas_call x1, Pallas kernels, attend(): pl.pallas_call(functools.partial(attention_kernel, heads, len(deltas), fu...  9.2 us
    dot_general x1, matrix products, body(): query = jnp.dot(scaled, query_matrix, preferred_element_type=f32)  8.9 us
    pallas_call x2, Pallas kernels, project_up(): pl.pallas_call(functools.partial(up_kernel, offset, members, stored), gri...  7.59 us
    unnamed x35, local copies, waits for them, and re-layouts  4.64 us
    pallas_call x2, Pallas kernels, project_down(): pl.pallas_call(functools.partial(down_kernel, offset, [places for _, plac...  3.85 us
  transfers between devices with their start and end apart: 28, of which 17 were waited for; matrix products, arithmetic and copies ran while one was open for 10% of the time, Pallas kernels for 12%

profile of v1, /device:TPU:0, one launch (start us, length us, event | category | flops | bytes accessed | tf_op | source)
XLA Modules:
  0.0 168.3 jit_solution(14795768238549847910)
XLA Ops:
  1.8 3.0 %collective-permute-start = (bf16[1,128,1024]{2,1,0:T(8,128)(2,1)S(1)}, bf16[1,128,1024]{2,1,0:T(8,128)(2,1)S(1)}, u32[]{:S(2)}, u32[]{:S(2)}) collective-permute-start(bf16[1,128,1024]{2,1,0:T(8,128)(2,1)S(1)} %fusion.5.refs_0_), channel_id=1, source_target_pairs={{0,16},{8,24},{16,0},{24,8},{1,17},{9,25},{17,1},{25,9},{2,18},{10... | collective-permute-start | bytes 786440 | tf_op jit(solution)/shard_map/ppermute | solution.py:40
  4.8 6.3 %collective-permute-done.refs_1_ = bf16[1,128,1024]{2,1,0:T(8,128)(2,1)S(1)} collective-permute-done((bf16[1,128,1024]{2,1,0:T(8,128)(2,1)S(1)}, bf16[1,128,1024]{2,1,0:T(8,128)(2,1)S(1)}, u32[]{:S(2)}, u32[]{:S(2)}) %collective-permute-start) | collective-permute-done | bytes 262176 | tf_op jit(solution)/shard_map/ppermute | solution.py:40
  21.0 2.7 %collective-permute-done.3 = bf16[256,128]{1,0:T(8,128)(2,1)S(1)} collective-permute-done((bf16[256,128]{1,0:T(8,128)(2,1)S(1)}, bf16[256,128]{1,0:T(8,128)(2,1)S(1)}, u32[]{:S(2)}, u32[]{:S(2)}) %collective-permute-start.3) | collective-permute-done | bytes 65568 | tf_op jit(solution)/shard_map/ppermute | solution.py:40
  25.6 8.9 %fusion.2.query_ref = f32[128,1024]{1,0:T(8,128)} fusion(bf16[8192,1024]{1,0:T(8,128)(2,1)} %param.19, bf16[128,8192]{1,0:T(8,128)(2,1)S(1)} %copy-done.9, f32[8192]{0:T(1024)S(1)} %convert_element_type.197), kind=kOutput, calls=%fused_computation.6 | convolution fusion | flops 2150629376 | bytes 19431424 | tf_op jit(solution)/shard_map/dot_general | solution.py:436
  34.6 2.8 %collective-permute-start.5 = (bf16[256,128]{1,0:T(8,128)(2,1)S(1)}, bf16[256,128]{1,0:T(8,128)(2,1)S(1)}, u32[]{:S(2)}, u32[]{:S(2)}) collective-permute-start(bf16[256,128]{1,0:T(8,128)(2,1)S(1)} %add_convert_fusion.10), channel_id=1, source_target_pairs={{0,6},{1,7},{2,4},{3,5},{4,2},{5,3},{6,0},{7,1},{8,14},{9,15},{10,... | collective-permute-start | bytes 196616 | tf_op jit(solution)/shard_map/ppermute | solution.py:40
  37.9 2.8 %collective-permute-done.5 = bf16[256,128]{1,0:T(8,128)(2,1)S(1)} collective-permute-done((bf16[256,128]{1,0:T(8,128)(2,1)S(1)}, bf16[256,128]{1,0:T(8,128)(2,1)S(1)}, u32[]{:S(2)}, u32[]{:S(2)}) %collective-permute-start.5) | collective-permute-done | bytes 65568 | tf_op jit(solution)/shard_map/ppermute | solution.py:40
  40.7 4.2 %up.2 = (bf16[2,128,1024]{2,1,0:T(8,128)(2,1)S(1)}, bf16[2,128,1024]{2,1,0:T(8,128)(2,1)}) custom-call(s32[32]{0:T(128)S(1)} %select_n.32.aid_ref, bf16[256,128]{1,0:T(8,128)(2,1)S(1)} %add_convert_fusion.9.rank_ref, bf16[8,1024,256]{2,1,0:T(8,128)(2,1)S(1)} %copy-done.1), custom_call_target="tpu_custom_call" | custom-call | flops 1073741824 | bytes 6000000 | tf_op jit(solution)/shard_map/up/pallas_call | solution.py:293
  53.0 4.5 %collective-permute-done.7.refs_2_ = bf16[1,128,1024]{2,1,0:T(8,128)(2,1)S(1)} collective-permute-done((bf16[1,128,1024]{2,1,0:T(8,128)(2,1)S(1)}, bf16[1,128,1024]{2,1,0:T(8,128)(2,1)S(1)}, u32[]{:S(2)}, u32[]{:S(2)}) %collective-permute-start.7) | collective-permute-done | bytes 262176 | tf_op jit(solution)/shard_map/ppermute | solution.py:40
  58.6 9.2 %attend.1.rows_ref = bf16[128,1024]{1,0:T(8,128)(2,1)S(1)} custom-call(s32[1,192]{1,0:T(1,128)S(1)} %copy-done.6, f32[128,1024]{1,0:T(8,128)S(1)} %copy-done.4, f32[128,1]{1,0:T(8,128)S(1)} %copy.18.inv_ref, bf16[1,128,1024]{2,1,0:T(8,128)(2,1)S(1)} %slice.96.refs_0_, bf16[1,128,1024]{2,1,0:T(8,128)(2,1)S(1)} %slice.126.refs_1_, ...), custom_call_target="tpu_custom_call" | custom-call | flops 400000000 | bytes 8000000 | tf_op jit(solution)/shard_map/attend/pallas_call | solution.py:195
  69.3 6.0 %collective-permute-done.11.refs_1_ = bf16[1,128,1024]{2,1,0:T(8,128)(2,1)S(1)} collective-permute-done((bf16[1,128,1024]{2,1,0:T(8,128)(2,1)S(1)}, bf16[1,128,1024]{2,1,0:T(8,128)(2,1)S(1)}, u32[]{:S(2)}, u32[]{:S(2)}) %collective-permute-start.11) | collective-permute-done | bytes 262176 | tf_op jit(solution)/shard_map/ppermute | solution.py:40
  80.4 2.7 %collective-permute-done.14 = bf16[256,128]{1,0:T(8,128)(2,1)S(1)} collective-permute-done((bf16[256,128]{1,0:T(8,128)(2,1)S(1)}, bf16[256,128]{1,0:T(8,128)(2,1)S(1)}, u32[]{:S(2)}, u32[]{:S(2)}) %collective-permute-start.14) | collective-permute-done | bytes 65568 | tf_op jit(solution)/shard_map/ppermute | solution.py:40
  84.2 4.1 %block_dot.7 = bf16[4,128,512]{2,1,0:T(8,128)(2,1)S(1)} custom-call(s32[4]{0:T(128)S(1)} %multiply_add_fusion.columns_ref, bf16[128,1024]{1,0:T(8,128)(2,1)S(1)} %attend.1.rows_ref, bf16[1024,8192]{1,0:T(8,128)(2,1)} %weight_ref.7), custom_call_target="tpu_custom_call" | custom-call | flops 536870912 | bytes 4718592 | tf_op jit(solution)/shard_map/block_dot/pallas_call | solution.py:316
  90.4 2.8 %collective-permute-start.16 = (bf16[256,128]{1,0:T(8,128)(2,1)S(1)}, bf16[256,128]{1,0:T(8,128)(2,1)S(1)}, u32[]{:S(2)}, u32[]{:S(2)}) collective-permute-start(bf16[256,128]{1,0:T(8,128)(2,1)S(1)} %add_convert_fusion.7), channel_id=1, source_target_pairs={{0,6},{1,7},{2,4},{3,5},{4,2},{5,3},{6,0},{7,1},{8,14},{9,15},{10,... | collective-permute-start | bytes 196616 | tf_op jit(solution)/shard_map/ppermute | solution.py:40
  93.2 4.1 %block_dot.5 = bf16[4,128,512]{2,1,0:T(8,128)(2,1)S(1)} custom-call(s32[4]{0:T(128)S(1)} %xor_multiply_fusion.columns_ref, bf16[128,1024]{1,0:T(8,128)(2,1)S(1)} %attend.1.rows_ref, bf16[1024,8192]{1,0:T(8,128)(2,1)} %weight_ref.7), custom_call_target="tpu_custom_call" | custom-call | flops 536870912 | bytes 4718592 | tf_op jit(solution)/shard_map/block_dot/pallas_call | solution.py:316
  98.9 4.1 %block_dot.6 = bf16[4,128,512]{2,1,0:T(8,128)(2,1)S(1)} custom-call(s32[4]{0:T(128)S(1)} %multiply_add_fusion.1.columns_ref, bf16[128,1024]{1,0:T(8,128)(2,1)S(1)} %attend.1.rows_ref, bf16[1024,8192]{1,0:T(8,128)(2,1)} %weight_ref.7), custom_call_target="tpu_custom_call" | custom-call | flops 536870912 | bytes 4718592 | tf_op jit(solution)/shard_map/block_dot/pallas_call | solution.py:316
  105.0 3.4 %up.3 = (bf16[2,128,1024]{2,1,0:T(8,128)(2,1)S(1)}, bf16[2,128,1024]{2,1,0:T(8,128)(2,1)S(1)}) custom-call(s32[32]{0:T(128)S(1)} %select_n.32.aid_ref, bf16[256,128]{1,0:T(8,128)(2,1)S(1)} %add_convert_fusion.6.rank_ref, bf16[8,1024,256]{2,1,0:T(8,128)(2,1)S(1)} %copy-done.2), custom_call_target="tpu_custom_call" | custom-call | flops 1073741824 | bytes 6000000 | tf_op jit(solution)/shard_map/up/pallas_call | solution.py:293
  108.5 4.1 %block_dot.4 = bf16[4,128,512]{2,1,0:T(8,128)(2,1)S(1)} custom-call(s32[4]{0:T(128)S(1)} %xor_multiply_fusion.1.columns_ref, bf16[128,1024]{1,0:T(8,128)(2,1)S(1)} %attend.1.rows_ref, bf16[1024,8192]{1,0:T(8,128)(2,1)} %weight_ref.7), custom_call_target="tpu_custom_call" | custom-call | flops 536870912 | bytes 4718592 | tf_op jit(solution)/shard_map/block_dot/pallas_call | solution.py:316
  115.7 8.1 %collective-permute-done.23 = bf16[2,128,512]{2,1,0:T(8,128)(2,1)S(1)} collective-permute-done((bf16[2,128,512]{2,1,0:T(8,128)(2,1)S(1)}, bf16[2,128,512]{2,1,0:T(8,128)(2,1)S(1)}, u32[]{:S(2)}, u32[]{:S(2)}) %collective-permute-start.23) | collective-permute-done | bytes 262176 | tf_op jit(solution)/shard_map/ppermute | solution.py:40
  130.3 4.6 %collective-permute-done.10 = bf16[1,128,512]{2,1,0:T(8,128)(2,1)S(1)} collective-permute-done((bf16[1,128,512]{2,1,0:T(8,128)(2,1)S(1)}, bf16[1,128,512]{2,1,0:T(8,128)(2,1)S(1)}, u32[]{:S(2)}, u32[]{:S(2)}) %collective-permute-start.10) | collective-permute-done | bytes 131104 | tf_op jit(solution)/shard_map/ppermute | solution.py:40
  139.3 2.9 %collective-permute-done.19 = bf16[1,128,512]{2,1,0:T(8,128)(2,1)S(1)} collective-permute-done((bf16[1,128,512]{2,1,0:T(8,128)(2,1)S(1)}, bf16[1,128,512]{2,1,0:T(8,128)(2,1)S(1)}, u32[]{:S(2)}, u32[]{:S(2)}) %collective-permute-start.19) | collective-permute-done | bytes 131104 | tf_op jit(solution)/shard_map/ppermute | solution.py:40
  143.9 2.7 %collective-permute-start.26 = (bf16[2,128,512]{2,1,0:T(8,128)(2,1)S(1)}, bf16[2,128,512]{2,1,0:T(8,128)(2,1)S(1)}, u32[]{:S(2)}, u32[]{:S(2)}) collective-permute-start(bf16[2,128,512]{2,1,0:T(8,128)(2,1)S(1)} %pad_maximum_fusion.3), channel_id=1, source_target_pairs={{0,6},{1,7},{2,4},{3,5},{4,2},{5,3},{6,0},{7,1},{8,14},{9,15},{10,... | collective-permute-start | bytes 786440 | tf_op jit(solution)/shard_map/ppermute | solution.py:40
  146.6 4.8 %collective-permute-done.20 = bf16[2,128,512]{2,1,0:T(8,128)(2,1)S(1)} collective-permute-done((bf16[2,128,512]{2,1,0:T(8,128)(2,1)S(1)}, bf16[2,128,512]{2,1,0:T(8,128)(2,1)S(1)}, u32[]{:S(2)}, u32[]{:S(2)}) %collective-permute-start.20) | collective-permute-done | bytes 262176 | tf_op jit(solution)/shard_map/ppermute | solution.py:40
  155.9 4.8 %collective-permute-done.21.refs_1_ = bf16[4,128,512]{2,1,0:T(8,128)(2,1)S(1)} collective-permute-done((bf16[4,128,512]{2,1,0:T(8,128)(2,1)S(1)}, bf16[4,128,512]{2,1,0:T(8,128)(2,1)S(1)}, u32[]{:S(2)}, u32[]{:S(2)}) %collective-permute-start.21) | collective-permute-done | bytes 524320 | tf_op jit(solution)/shard_map/ppermute | solution.py:40
  160.7 5.5 %collective-permute-done.27.refs_3_ = bf16[4,128,512]{2,1,0:T(8,128)(2,1)S(1)} collective-permute-done((bf16[4,128,512]{2,1,0:T(8,128)(2,1)S(1)}, bf16[4,128,512]{2,1,0:T(8,128)(2,1)S(1)}, u32[]{:S(2)}, u32[]{:S(2)}) %collective-permute-start.27) | collective-permute-done | bytes 524320 | tf_op jit(solution)/shard_map/ppermute | solution.py:40
  (124 shorter events, 58.7 us)
Async XLA Ops:
  1.8 9.3 %collective-permute-start = (bf16[1,128,1024]{2,1,0:T(8,128)(2,1)S(1)}, bf16[1,128,1024]{2,1,0:T(8,128)(2,1)S(1)}, u32[]{:S(2)}, u32[]{:S(2)}) collective-permute-start(bf16[1,128,1024]{2,1,0:T(8,128)(2,1)S(1)} %fusion.5.refs_0_), channel_id=1, source_target_pairs={{0,16},{8,24},{16,0},{24,8},{1,17},{9,25},{17,1},{25,9},{2,18},{10... | collective-permute-start | bytes 786440 | tf_op jit(solution)/shard_map/ppermute | solution.py:40
  4.8 10.2 %collective-permute-start.1 = (bf16[1,128,1024]{2,1,0:T(8,128)(2,1)S(1)}, bf16[1,128,1024]{2,1,0:T(8,128)(2,1)S(1)}, u32[]{:S(2)}, u32[]{:S(2)}) collective-permute-start(bf16[1,128,1024]{2,1,0:T(8,128)(2,1)S(1)} %fusion.5.refs_0_), channel_id=1, source_target_pairs={{0,8},{8,0},{16,24},{24,16},{1,9},{9,1},{17,25},{25,17},{2,10},{10... | collective-permute-start | bytes 786440 | tf_op jit(solution)/shard_map/ppermute | solution.py:40
  19.1 4.6 %collective-permute-start.3 = (bf16[256,128]{1,0:T(8,128)(2,1)S(1)}, bf16[256,128]{1,0:T(8,128)(2,1)S(1)}, u32[]{:S(2)}, u32[]{:S(2)}) collective-permute-start(bf16[256,128]{1,0:T(8,128)(2,1)S(1)} %down.2), channel_id=1, source_target_pairs={{0,1},{1,0},{2,3},{3,2},{4,5},{5,4},{6,7},{7,6},{8,9},{9,8},{10,11... | collective-permute-start | bytes 196616 | tf_op jit(solution)/shard_map/ppermute | solution.py:40
  23.8 10.8 %collective-permute-start.4 = (bf16[256,128]{1,0:T(8,128)(2,1)S(1)}, bf16[256,128]{1,0:T(8,128)(2,1)S(1)}, u32[]{:S(2)}, u32[]{:S(2)}) collective-permute-start(bf16[256,128]{1,0:T(8,128)(2,1)S(1)} %add_convert_fusion.11), channel_id=1, source_target_pairs={{0,2},{1,3},{2,0},{3,1},{4,6},{5,7},{6,4},{7,5},{8,10},{9,11},{10,... | collective-permute-start | bytes 196616 | tf_op jit(solution)/shard_map/ppermute | solution.py:40
  34.6 6.1 %collective-permute-start.5 = (bf16[256,128]{1,0:T(8,128)(2,1)S(1)}, bf16[256,128]{1,0:T(8,128)(2,1)S(1)}, u32[]{:S(2)}, u32[]{:S(2)}) collective-permute-start(bf16[256,128]{1,0:T(8,128)(2,1)S(1)} %add_convert_fusion.10), channel_id=1, source_target_pairs={{0,6},{1,7},{2,4},{3,5},{4,2},{5,3},{6,0},{7,1},{8,14},{9,15},{10,... | collective-permute-start | bytes 196616 | tf_op jit(solution)/shard_map/ppermute | solution.py:40
  49.1 8.4 %collective-permute-start.7 = (bf16[1,128,1024]{2,1,0:T(8,128)(2,1)S(1)}, bf16[1,128,1024]{2,1,0:T(8,128)(2,1)S(1)}, u32[]{:S(2)}, u32[]{:S(2)}) collective-permute-start(bf16[1,128,1024]{2,1,0:T(8,128)(2,1)S(1)} %add_convert_fusion.3), channel_id=1, source_target_pairs={{0,16},{8,24},{16,0},{24,8},{1,17},{9,25},{17,1},{25,9},{2,18},{10... | collective-permute-start | bytes 786440 | tf_op jit(solution)/shard_map/ppermute | solution.py:40
  67.8 7.6 %collective-permute-start.11 = (bf16[1,128,1024]{2,1,0:T(8,128)(2,1)S(1)}, bf16[1,128,1024]{2,1,0:T(8,128)(2,1)S(1)}, u32[]{:S(2)}, u32[]{:S(2)}) collective-permute-start(bf16[1,128,1024]{2,1,0:T(8,128)(2,1)S(1)} %bitcast.25), channel_id=1, source_target_pairs={{0,16},{8,24},{16,0},{24,8},{1,17},{9,25},{17,1},{25,9},{2,18},{10... | collective-permute-start | bytes 786440 | tf_op jit(solution)/shard_map/ppermute | solution.py:40
  69.3 6.0 %collective-permute-start.12 = (bf16[1,128,1024]{2,1,0:T(8,128)(2,1)S(1)}, bf16[1,128,1024]{2,1,0:T(8,128)(2,1)S(1)}, u32[]{:S(2)}, u32[]{:S(2)}) collective-permute-start(bf16[1,128,1024]{2,1,0:T(8,128)(2,1)S(1)} %bitcast.26), channel_id=1, source_target_pairs={{0,8},{8,0},{16,24},{24,16},{1,9},{9,1},{17,25},{25,17},{2,10},{10... | collective-permute-start | bytes 786440 | tf_op jit(solution)/shard_map/ppermute | solution.py:40
  83.1 7.2 %collective-permute-start.15 = (bf16[256,128]{1,0:T(8,128)(2,1)S(1)}, bf16[256,128]{1,0:T(8,128)(2,1)S(1)}, u32[]{:S(2)}, u32[]{:S(2)}) collective-permute-start(bf16[256,128]{1,0:T(8,128)(2,1)S(1)} %add_convert_fusion.8), channel_id=1, source_target_pairs={{0,2},{1,3},{2,0},{3,1},{4,6},{5,7},{6,4},{7,5},{8,10},{9,11},{10,... | collective-permute-start | bytes 196616 | tf_op jit(solution)/shard_map/ppermute | solution.py:40
  88.3 24.3 %collective-permute-start.22 = (bf16[4,128,512]{2,1,0:T(8,128)(2,1)S(1)}, bf16[4,128,512]{2,1,0:T(8,128)(2,1)S(1)}, u32[]{:S(2)}, u32[]{:S(2)}) collective-permute-start(bf16[4,128,512]{2,1,0:T(8,128)(2,1)S(1)} %block_dot.7), channel_id=1, source_target_pairs={{0,2},{1,3},{2,0},{3,1},{4,6},{5,7},{6,4},{7,5},{8,10},{9,11},{10,... | collective-permute-start | bytes 1572872 | tf_op jit(solution)/shard_map/ppermute | solution.py:40
  90.4 14.6 %collective-permute-start.16 = (bf16[256,128]{1,0:T(8,128)(2,1)S(1)}, bf16[256,128]{1,0:T(8,128)(2,1)S(1)}, u32[]{:S(2)}, u32[]{:S(2)}) collective-permute-start(bf16[256,128]{1,0:T(8,128)(2,1)S(1)} %add_convert_fusion.7), channel_id=1, source_target_pairs={{0,6},{1,7},{2,4},{3,5},{4,2},{5,3},{6,0},{7,1},{8,14},{9,15},{10,... | collective-permute-start | bytes 196616 | tf_op jit(solution)/shard_map/ppermute | solution.py:40
  97.3 16.6 %collective-permute-start.8 = (bf16[4,128,512]{2,1,0:T(8,128)(2,1)S(1)}, bf16[4,128,512]{2,1,0:T(8,128)(2,1)S(1)}, u32[]{:S(2)}, u32[]{:S(2)}) collective-permute-start(bf16[4,128,512]{2,1,0:T(8,128)(2,1)S(1)} %block_dot.5), channel_id=1, source_target_pairs={{0,1},{1,0},{2,3},{3,2},{4,5},{5,4},{6,7},{7,6},{8,9},{9,8},{10,11... | collective-permute-start | bytes 1572872 | tf_op jit(solution)/shard_map/ppermute | solution.py:40
  108.5 5.5 %collective-permute-start.17 = (bf16[2,128,1024]{2,1,0:T(8,128)(2,1)S(1)}, bf16[2,128,1024]{2,1,0:T(8,128)(2,1)S(1)}, u32[]{:S(2)}, u32[]{:S(2)}) collective-permute-start(bf16[2,128,1024]{2,1,0:T(8,128)(2,1)S(1)} %get-tuple-element.18), channel_id=1, source_target_pairs={{0,8},{8,0},{16,24},{24,16},{1,9},{9,1},{17,25},{25,17},{2,10},{10... | collective-permute-start | bytes 1572872 | tf_op jit(solution)/shard_map/ppermute | solution.py:40
  112.7 11.1 %collective-permute-start.23 = (bf16[2,128,512]{2,1,0:T(8,128)(2,1)S(1)}, bf16[2,128,512]{2,1,0:T(8,128)(2,1)S(1)}, u32[]{:S(2)}, u32[]{:S(2)}) collective-permute-start(bf16[2,128,512]{2,1,0:T(8,128)(2,1)S(1)} %add_convert_fusion), channel_id=1, source_target_pairs={{0,6},{1,7},{2,4},{3,5},{4,2},{5,3},{6,0},{7,1},{8,14},{9,15},{10,... | collective-permute-start | bytes 786440 | tf_op jit(solution)/shard_map/ppermute | solution.py:40
  113.9 14.1 %collective-permute-start.9 = (bf16[2,128,512]{2,1,0:T(8,128)(2,1)S(1)}, bf16[2,128,512]{2,1,0:T(8,128)(2,1)S(1)}, u32[]{:S(2)}, u32[]{:S(2)}) collective-permute-start(bf16[2,128,512]{2,1,0:T(8,128)(2,1)S(1)} %add_convert_fusion.2), channel_id=1, source_target_pairs={{0,2},{1,3},{2,0},{3,1},{4,6},{5,7},{6,4},{7,5},{8,10},{9,11},{10,... | collective-permute-start | bytes 786440 | tf_op jit(solution)/shard_map/ppermute | solution.py:40
  114.1 16.1 %collective-permute-start.18 = (bf16[1,128,1024]{2,1,0:T(8,128)(2,1)S(1)}, bf16[1,128,1024]{2,1,0:T(8,128)(2,1)S(1)}, u32[]{:S(2)}, u32[]{:S(2)}) collective-permute-start(bf16[1,128,1024]{2,1,0:T(8,128)(2,1)S(1)} %add_convert_fusion.1), channel_id=1, source_target_pairs={{0,16},{8,24},{16,0},{24,8},{1,17},{9,25},{17,1},{25,9},{2,18},{10... | collective-permute-start | bytes 786440 | tf_op jit(solution)/shard_map/ppermute | solution.py:40
  123.9 6.5 %collective-permute-start.24 = (bf16[1,128,512]{2,1,0:T(8,128)(2,1)S(1)}, bf16[1,128,512]{2,1,0:T(8,128)(2,1)S(1)}, u32[]{:S(2)}, u32[]{:S(2)}) collective-permute-start(bf16[1,128,512]{2,1,0:T(8,128)(2,1)S(1)} %add_convert_fusion.4), channel_id=1, source_target_pairs={{0,1},{1,0},{2,3},{3,2},{4,5},{5,4},{6,7},{7,6},{8,9},{9,8},{10,11... | collective-permute-start | bytes 393224 | tf_op jit(solution)/shard_map/ppermute | solution.py:40
  128.1 6.8 %collective-permute-start.10 = (bf16[1,128,512]{2,1,0:T(8,128)(2,1)S(1)}, bf16[1,128,512]{2,1,0:T(8,128)(2,1)S(1)}, u32[]{:S(2)}, u32[]{:S(2)}) collective-permute-start(bf16[1,128,512]{2,1,0:T(8,128)(2,1)S(1)} %add_convert_fusion.5), channel_id=1, source_target_pairs={{0,6},{1,7},{2,4},{3,5},{4,2},{5,3},{6,0},{7,1},{8,14},{9,15},{10,... | collective-permute-start | bytes 393224 | tf_op jit(solution)/shard_map/ppermute | solution.py:40
  135.2 7.0 %collective-permute-start.19 = (bf16[1,128,512]{2,1,0:T(8,128)(2,1)S(1)}, bf16[1,128,512]{2,1,0:T(8,128)(2,1)S(1)}, u32[]{:S(2)}, u32[]{:S(2)}) collective-permute-start(bf16[1,128,512]{2,1,0:T(8,128)(2,1)S(1)} %get-tuple-element.20), channel_id=1, source_target_pairs={{0,6},{1,7},{2,4},{3,5},{4,2},{5,3},{6,0},{7,1},{8,14},{9,15},{10,... | collective-permute-start | bytes 393224 | tf_op jit(solution)/shard_map/ppermute | solution.py:40
  137.9 6.0 %collective-permute-start.25 = (bf16[1,128,512]{2,1,0:T(8,128)(2,1)S(1)}, bf16[1,128,512]{2,1,0:T(8,128)(2,1)S(1)}, u32[]{:S(2)}, u32[]{:S(2)}) collective-permute-start(bf16[1,128,512]{2,1,0:T(8,128)(2,1)S(1)} %get-tuple-element.19), channel_id=1, source_target_pairs={{0,1},{1,0},{2,3},{3,2},{4,5},{5,4},{6,7},{7,6},{8,9},{9,8},{10,11... | collective-permute-start | bytes 393224 | tf_op jit(solution)/shard_map/ppermute | solution.py:40
  142.2 9.2 %collective-permute-start.20 = (bf16[2,128,512]{2,1,0:T(8,128)(2,1)S(1)}, bf16[2,128,512]{2,1,0:T(8,128)(2,1)S(1)}, u32[]{:S(2)}, u32[]{:S(2)}) collective-permute-start(bf16[2,128,512]{2,1,0:T(8,128)(2,1)S(1)} %pad_maximum_fusion.2), channel_id=1, source_target_pairs={{0,2},{1,3},{2,0},{3,1},{4,6},{5,7},{6,4},{7,5},{8,10},{9,11},{10,... | collective-permute-start | bytes 786440 | tf_op jit(solution)/shard_map/ppermute | solution.py:40
  143.9 11.1 %collective-permute-start.26 = (bf16[2,128,512]{2,1,0:T(8,128)(2,1)S(1)}, bf16[2,128,512]{2,1,0:T(8,128)(2,1)S(1)}, u32[]{:S(2)}, u32[]{:S(2)}) collective-permute-start(bf16[2,128,512]{2,1,0:T(8,128)(2,1)S(1)} %pad_maximum_fusion.3), channel_id=1, source_target_pairs={{0,6},{1,7},{2,4},{3,5},{4,2},{5,3},{6,0},{7,1},{8,14},{9,15},{10,... | collective-permute-start | bytes 786440 | tf_op jit(solution)/shard_map/ppermute | solution.py:40
  151.5 9.2 %collective-permute-start.21 = (bf16[4,128,512]{2,1,0:T(8,128)(2,1)S(1)}, bf16[4,128,512]{2,1,0:T(8,128)(2,1)S(1)}, u32[]{:S(2)}, u32[]{:S(2)}) collective-permute-start(bf16[4,128,512]{2,1,0:T(8,128)(2,1)S(1)} %pad_maximum_fusion.refs_0_), channel_id=1, source_target_pairs={{0,1},{1,0},{2,3},{3,2},{4,5},{5,4},{6,7},{7,6},{8,9},{9,8},{10,11... | collective-permute-start | bytes 1572872 | tf_op jit(solution)/shard_map/ppermute | solution.py:40
  155.1 11.1 %collective-permute-start.27 = (bf16[4,128,512]{2,1,0:T(8,128)(2,1)S(1)}, bf16[4,128,512]{2,1,0:T(8,128)(2,1)S(1)}, u32[]{:S(2)}, u32[]{:S(2)}) collective-permute-start(bf16[4,128,512]{2,1,0:T(8,128)(2,1)S(1)} %pad_maximum_fusion.1.refs_2_), channel_id=1, source_target_pairs={{0,2},{1,3},{2,0},{3,1},{4,6},{5,7},{6,4},{7,5},{8,10},{9,11},{10,... | collective-permute-start | bytes 1572872 | tf_op jit(solution)/shard_map/ppermute | solution.py:40
  (21 other events, 350.4 us)

commit v2 on v1

v2 whole, which is shorter than its diff:
```python
import functools
import math

import jax
import jax.numpy as jnp
from jax import lax
from jax.experimental import pallas as pl
from jax.experimental.pallas import tpu as pltpu
from jax.sharding import PartitionSpec as P


KVH = 8
HD = 128
SEG = 16
PAGES_MAX = 8
LANES = 128
SLOTS = 8

adapter_scale = 2.0
norm_eps = 1e-05
rope_base = 500000.0
hidden_mask = -1e30

f32 = jnp.float32
bf16 = jnp.bfloat16
VMEM = pl.BlockSpec(memory_space=pltpu.VMEM)
SMEM = pl.BlockSpec(memory_space=pltpu.SMEM)
ANY = pl.BlockSpec(memory_space=pl.ANY)
NT = (((1,), (1,)), ((), ()))
TN = (((0,), (0,)), ((), ()))


def cost(flops, traffic):
    return pl.CostEstimate(flops=int(flops), bytes_accessed=int(traffic), transcendentals=0)


def params(mib):
    return pltpu.CompilerParams(vmem_limit_bytes=mib << 20)


def flip(value, axis, bits):
    return lax.ppermute(value, axis, [(i, i ^ bits) for i in range(lax.axis_size(axis))])


def tables(positions):
    half = HD // 2
    frequency = rope_base ** (-(jnp.arange(half).astype(f32) * 2.0) / HD)
    angles = positions[:, None] * frequency[None, :]
    cosine, sine = jnp.cos(angles), jnp.sin(angles)
    return jnp.concatenate([cosine, cosine], 1), jnp.concatenate([-sine, sine], 1)


def prep_kernel(half_size, counts_ref, trims_ref, owner_ref, mask_ref, row_ref):
    slots, rows = owner_ref.shape
    counts = counts_ref[...].astype(f32)
    trims = trims_ref[...].astype(f32)
    before = lax.broadcasted_iota(jnp.int32, (rows, rows), 0)
    after = lax.broadcasted_iota(jnp.int32, (rows, rows), 1)
    earlier = jnp.where(before < after, 1.0, 0.0).astype(bf16)
    start = jnp.dot(
        jnp.broadcast_to(counts, (8, rows)).astype(bf16), earlier, preferred_element_type=f32
    )[0:1]
    end = start + counts
    slot = lax.broadcasted_iota(jnp.int32, (slots, rows), 0).astype(f32)
    owner = jnp.where((slot >= start) & (slot < end), 1.0, 0.0)
    owner_ref[...] = owner
    last = jnp.where(slot == end - 1.0, trims, 0.0)
    used = half_size - jnp.sum(last, axis=1, keepdims=True)
    row = lax.broadcasted_iota(jnp.int32, (slots, rows), 1).astype(f32)
    row_ref[...] = jnp.broadcast_to(
        jnp.sum(owner * row, axis=1, keepdims=True), row_ref.shape
    )
    shape = mask_ref.shape
    place = lax.broadcasted_iota(jnp.int32, shape, 0) % SLOTS
    column = lax.broadcasted_iota(jnp.int32, shape, 1)
    fits = (column // half_size == place) & ((column % half_size).astype(f32) < used)
    mask_ref[...] = jnp.where(fits, 0.0, hidden_mask)


def prepare(counts, trims, slots, half_size):
    rows = counts.shape[1]
    return pl.pallas_call(
        functools.partial(prep_kernel, half_size),
        out_shape=(
            jax.ShapeDtypeStruct((slots, rows), f32),
            jax.ShapeDtypeStruct((slots, SLOTS * half_size), f32),
            jax.ShapeDtypeStruct((slots, LANES), f32),
        ),
        in_specs=[VMEM, VMEM],
        out_specs=(VMEM, VMEM, VMEM),
        compiler_params=params(4),
        cost_estimate=cost(1e6, 5e5),
        name="prep",
    )(counts, trims)


def attention_kernel(
    heads, extra, fused, order_ref, query_ref, inv_ref, *refs
):
    deltas, refs = refs[:extra], refs[extra:]
    cos_ref, sin_ref, owner_ref, mask_ref, row_ref, kv_ref = refs[:6]
    outs = refs[6:-4]
    q_scr, o_scr, m_scr, l_scr = refs[-4:]
    slots = owner_ref.shape[0]
    steps = slots // SLOTS
    half_size = kv_ref.shape[2]
    owner = owner_ref[...]
    owner_low = owner.astype(bf16)
    for head in range(heads):
        lanes = slice(head * HD, (head + 1) * HD)
        value = query_ref[:, lanes]
        if fused:
            for ref in deltas:
                value = value + adapter_scale * ref[0, :, lanes].astype(f32)
            value = value * inv_ref[...]
            value = value * cos_ref[...] + pltpu.roll(value, HD // 2, 1) * sin_ref[...]
        spread = jnp.dot(owner_low, value.astype(bf16), preferred_element_type=f32)
        q_scr[:, head * SLOTS : (head + 1) * SLOTS, :] = spread.reshape(steps, SLOTS, HD)

    def step(b, carry):
        pages = [kv_ref[order_ref[0, b * SLOTS + i], 0] for i in range(SLOTS)]
        keys = jnp.concatenate([page[:, :HD] for page in pages], axis=0)
        values = jnp.concatenate([page[:, HD:] for page in pages], axis=0)
        scores = lax.dot_general(
            q_scr[b].astype(bf16), keys, NT, preferred_element_type=f32
        ) * (1.0 / math.sqrt(HD))
        width = SLOTS * half_size
        mask = mask_ref[pl.ds(pl.multiple_of(b * SLOTS, SLOTS), SLOTS), :]
        scores = (scores.reshape(heads, SLOTS, width) + mask[None]).reshape(heads * SLOTS, width)
        top = jnp.max(scores, axis=1, keepdims=True)
        weights = jnp.exp(scores - top).astype(bf16)
        total = jnp.sum(weights.astype(f32), axis=1, keepdims=True)
        o_scr[b] = jnp.dot(weights, values, preferred_element_type=f32)
        m_scr[b] = jnp.broadcast_to(top, (heads * SLOTS, LANES))
        l_scr[b] = jnp.broadcast_to(total, (heads * SLOTS, LANES))
        return carry

    lax.fori_loop(0, steps, step, 0, unroll=4 if steps % 4 == 0 else 1)

    lane = lax.broadcasted_iota(jnp.int32, (slots, LANES), 1)
    tops = jnp.zeros((slots, LANES), f32)
    totals = jnp.zeros((slots, LANES), f32)
    for head in range(heads):
        part = slice(head * SLOTS, (head + 1) * SLOTS)
        tops = jnp.where(lane == head, m_scr[:, part, :].reshape(slots, LANES), tops)
        totals = jnp.where(lane == head, l_scr[:, part, :].reshape(slots, LANES), totals)
    row = row_ref[...]
    joint = tops
    distance = 1
    while distance < PAGES_MAX:
        for shift in (distance, slots - distance):
            same = pltpu.roll(row, shift, 0) == row
            joint = jnp.where(same, jnp.maximum(joint, pltpu.roll(joint, shift, 0)), joint)
        distance *= 2
    factor = jnp.exp(tops - joint)
    dot = functools.partial(
        lax.dot_general,
        dimension_numbers=TN,
        precision=lax.Precision.HIGHEST,
        preferred_element_type=f32,
    )
    denom = dot(owner, totals * factor)
    for head in range(heads):
        part = slice(head * SLOTS, (head + 1) * SLOTS)
        lanes = slice(head * HD, (head + 1) * HD)
        value = o_scr[:, part, :].reshape(slots, HD) * factor[:, head : head + 1]
        numer = dot(owner, value)
        if fused:
            outs[0][:, lanes] = (numer / denom[:, head : head + 1]).astype(bf16)
        else:
            outs[0][:, lanes] = numer
    if not fused:
        previous = pltpu.roll(row, 1, 0) == row
        first = jnp.where(previous, 0.0, owner)
        outs[1][...] = dot(first, joint)
        outs[2][...] = denom


def attend(query, inv, deltas, cosine, sine, owner, mask, row, order, pages, fused):
    rows = query.shape[0]
    slots = owner.shape[0]
    heads = query.shape[1] // HD
    width = query.shape[1]
    if fused:
        out_shape = (jax.ShapeDtypeStruct((rows, width), bf16),)
    else:
        small = jax.ShapeDtypeStruct((rows, LANES), f32)
        out_shape = (jax.ShapeDtypeStruct((rows, width), f32), small, small)
    first = pl.BlockSpec((1, rows, width), lambda i: (0, 0, 0))

    def whole(value):
        return pl.BlockSpec(value.shape, lambda i, n=value.ndim: (0,) * n)

    steps = slots // SLOTS
    scratch = pltpu.VMEM((steps, heads * SLOTS, LANES), f32)
    fixed = (cosine, sine, owner, mask, row, pages)
    return pl.pallas_call(
        functools.partial(attention_kernel, heads, len(deltas), fused),
        grid=(1,),
        out_shape=out_shape,
        in_specs=[SMEM, whole(query), whole(inv)]
        + [first] * len(deltas)
        + [whole(value) for value in fixed],
        out_specs=tuple(pl.BlockSpec(s.shape, lambda i: (0, 0)) for s in out_shape),
        scratch_shapes=[scratch] * 4,
        compiler_params=params(24),
        cost_estimate=cost(4e8, 8e6),
        name="attend",
    )(order, query, inv, *deltas, *fixed)


def capacity_of(members, seg_count):
    return max(2, (2 * seg_count + members - 1) // members)


def own_kernel(hidden_ref, gain_ref, out_ref, rows_scr, gain_scr, sem):
    width = out_ref.shape[2]
    start = pl.multiple_of(lax.axis_index("tensor") * width, LANES)
    rows = pltpu.make_async_copy(hidden_ref.at[:, pl.ds(start, width)], rows_scr, sem.at[0])
    gain = pltpu.make_async_copy(gain_ref.at[:, pl.ds(start, width)], gain_scr, sem.at[1])
    rows.start()
    gain.start()
    rows.wait()
    gain.wait()
    out_ref[0] = (rows_scr[...].astype(f32) * gain_scr[...].astype(f32)).astype(bf16)


def scale_own(hidden, gain, width):
    rows = hidden.shape[0]
    return pl.pallas_call(
        own_kernel,
        out_shape=jax.ShapeDtypeStruct((1, rows, width), bf16),
        in_specs=[ANY, ANY],
        out_specs=VMEM,
        scratch_shapes=[
            pltpu.VMEM((rows, width), bf16),
            pltpu.VMEM((1, width), bf16),
            pltpu.SemaphoreType.DMA((2,)),
        ],
        compiler_params=params(8),
        cost_estimate=cost(rows * width, 4 * rows * width),
        name="own",
    )(hidden, gain)


def query_kernel(hidden_ref, gain_ref, weight_ref, store_ref, out_ref, inv_ref, kept_ref, *scr):
    h_scr, w_scr, sem, store_sem = scr
    chunks = h_scr.shape[0]
    depth = h_scr.shape[2]
    copies = []
    for i in range(chunks):
        span = pl.ds(i * depth, depth)
        copies.append(
            (
                pltpu.make_async_copy(hidden_ref.at[:, span], h_scr.at[i], sem.at[2 * i]),
                pltpu.make_async_copy(weight_ref.at[span], w_scr.at[i], sem.at[2 * i + 1]),
            )
        )
    for pair in copies:
        for copy in pair:
            copy.start()
    stores = [
        pltpu.make_async_copy(store_ref.at[a], kept_ref.at[a], store_sem.at[a])
        for a in range(store_ref.shape[0])
    ]
    for copy in stores:
        copy.start()
    squares = None
    for i, pair in enumerate(copies):
        for copy in pair:
            copy.wait()
        wide = h_scr[i].astype(f32)
        power = jnp.sum(wide * wide, axis=1, keepdims=True)
        squares = power if i == 0 else squares + power
        scaled = (wide * gain_ref[:, i * depth : (i + 1) * depth].astype(f32)).astype(bf16)
        product = jnp.dot(scaled, w_scr[i], preferred_element_type=f32)
        if i == 0:
            out_ref[...] = product
        else:
            out_ref[...] += product
    inv_ref[...] = lax.rsqrt(squares / (chunks * depth) + norm_eps)
    for copy in stores:
        copy.wait()


def project_query(hidden, gain, weight, store):
    rows, model = hidden.shape
    width = weight.shape[1]
    chunks = 8
    depth = model // chunks
    return pl.pallas_call(
        query_kernel,
        out_shape=(
            pltpu.VMEM((rows, width), f32),
            pltpu.VMEM((rows, 1), f32),
            pltpu.VMEM(store.shape, bf16),
        ),
        in_specs=[ANY, VMEM, ANY, ANY],
        out_specs=(VMEM, VMEM, VMEM),
        scratch_shapes=[
            pltpu.VMEM((chunks, rows, depth), bf16),
            pltpu.VMEM((chunks, depth, width), bf16),
            pltpu.SemaphoreType.DMA((2 * chunks,)),
            pltpu.SemaphoreType.DMA((store.shape[0],)),
        ],
        compiler_params=params(32),
        cost_estimate=cost(2 * rows * weight.size, 2 * (weight.size + store.size + hidden.size)),
        name="query",
    )(hidden, gain, weight, store)


def fetch_kernel(first, weight_ref, kept_ref, sem):
    copies = []
    pieces = sem.shape[0]
    depth = kept_ref.shape[0] // pieces
    for i in range(pieces):
        copies.append(
            pltpu.make_async_copy(
                weight_ref.at[pl.ds(first + i * depth, depth)],
                kept_ref.at[pl.ds(i * depth, depth)],
                sem.at[i],
            )
        )
    for copy in copies:
        copy.start()
    for copy in copies:
        copy.wait()


def fetch(weight, first, depth):
    return pl.pallas_call(
        functools.partial(fetch_kernel, first),
        out_shape=pltpu.VMEM((depth, weight.shape[1]), bf16),
        in_specs=[ANY],
        out_specs=VMEM,
        scratch_shapes=[pltpu.SemaphoreType.DMA((4,))],
        compiler_params=params(1),
        cost_estimate=cost(0, 2 * depth * weight.shape[1]),
        name="fetch",
    )(weight)


def block_kernel(offsets, addends, parts, rows_ref, *refs):
    weights, refs = refs[:parts], refs[parts:]
    added, outs = refs[:addends], refs[addends:]
    width = outs[0].shape[1]
    depth = rows_ref.shape[1] // parts
    index = lax.axis_index("tensor")
    for i, offset in enumerate(offsets):
        start = pl.multiple_of((index ^ offset) * width, LANES)
        total = None
        for p, weight_ref in enumerate(weights):
            product = jnp.dot(
                rows_ref[:, p * depth : (p + 1) * depth],
                weight_ref[:, pl.ds(start, width)],
                preferred_element_type=f32,
            )
            total = product if p == 0 else total + product
        if i == 0:
            for ref in added:
                total = total + ref[...].astype(f32)
        outs[i][...] = total.astype(bf16)


def block_dot(offsets, rows, weights, added=()):
    width = rows.shape[1]
    out = jax.ShapeDtypeStruct((rows.shape[0], width), bf16)
    count = len(offsets)
    return pl.pallas_call(
        functools.partial(block_kernel, offsets, len(added), len(weights)),
        out_shape=(out,) * count,
        in_specs=[VMEM] * (1 + len(weights) + len(added)),
        out_specs=(VMEM,) * count,
        compiler_params=params(8),
        cost_estimate=cost(2 * count * rows.size * width, 4 * count * rows.size),
        name="block_dot",
    )(rows, *weights, *added)


def finish_kernel(sums, deltas, parts, rows_ref, *refs):
    weights, refs = refs[:parts], refs[parts:]
    added, refs = refs[:sums], refs[sums:]
    returned, (hidden_ref, out_ref, h_scr, sem) = refs[:deltas], refs[deltas:]
    width = out_ref.shape[1]
    depth = rows_ref.shape[1] // parts
    start = pl.multiple_of(lax.axis_index("tensor") * width, LANES)
    copy = pltpu.make_async_copy(hidden_ref.at[:, pl.ds(start, width)], h_scr, sem)
    copy.start()
    total = None
    for p, weight_ref in enumerate(weights):
        product = jnp.dot(
            rows_ref[:, p * depth : (p + 1) * depth],
            weight_ref[:, pl.ds(start, width)],
            preferred_element_type=f32,
        )
        total = product if p == 0 else total + product
    for ref in added:
        total = total + ref[...].astype(f32)
    delta = returned[0][0].astype(f32)
    for ref in returned[1:]:
        delta = delta + ref[0].astype(f32)
    copy.wait()
    out_ref[...] = (h_scr[...].astype(f32) + (total + adapter_scale * delta)).astype(bf16)


def finish(rows, weights, added, deltas, hidden):
    width = rows.shape[1]
    return pl.pallas_call(
        functools.partial(finish_kernel, len(added), len(deltas), len(weights)),
        out_shape=jax.ShapeDtypeStruct(rows.shape, bf16),
        in_specs=[VMEM] * (1 + len(weights) + len(added) + len(deltas)) + [ANY],
        out_specs=VMEM,
        scratch_shapes=[pltpu.VMEM(rows.shape, bf16), pltpu.SemaphoreType.DMA],
        compiler_params=params(8),
        cost_estimate=cost(2 * rows.size * width, 8 * rows.size),
        name="finish",
    )(rows, *weights, *added, *deltas, hidden)


def served(route_ref, slot_ref, members, seg_count, capacity):
    group = lax.axis_index("group")
    table = []
    for j in range(members):
        base = (group ^ j) * seg_count
        count = jnp.int32(0)
        for k in range(seg_count):
            here = route_ref[base + k] == group
            index = jnp.where(here, slot_ref[base + k], -1)
            place = jnp.where(here, jnp.minimum(count, capacity - 1), capacity)
            table.append((index, place))
            count = count + here.astype(jnp.int32)
    return table


def down_kernel(offset, places, capacity, route_ref, slot_ref, *refs):
    inputs, (store_ref, out_ref, y_scr, c_scr) = refs[: len(places)], refs[len(places) :]
    stored = store_ref.shape[0]
    members = sum(len(group) for group in places)
    rows = inputs[0].shape[1]
    seg_count = rows // SEG
    half = LANES // 2
    c_scr[...] = jnp.zeros_like(c_scr)
    for ref, group in zip(inputs, places):
        for i, j in enumerate(group):
            for a in range(0, stored, 2):
                pair = jnp.concatenate(
                    [store_ref[a, :, :LANES], store_ref[a + 1, :, :LANES]], axis=1
                )
                result = jnp.dot(ref[i], pair, preferred_element_type=f32)
                y_scr[a, j * rows : (j + 1) * rows, :] = result[:, :LANES]
                y_scr[a + 1, j * rows : (j + 1) * rows, :] = result[:, LANES:]
    table = served(route_ref, slot_ref, members, seg_count, capacity)
    for j in range(members):
        for k in range(seg_count):
            index, place = table[j * seg_count + k]
            c_scr[j, pl.ds(pl.multiple_of(place * SEG, SEG), SEG), :] = y_scr[
                jnp.maximum(index, 0), pl.ds(j * rows + k * SEG, SEG), :
            ]
    used = capacity * SEG
    left = lax.broadcasted_iota(jnp.int32, (used, LANES), 1) < half
    for j in range(0, members, 2):
        even, odd = c_scr[j, :used], c_scr[j + 1, :used]
        if offset:
            even = pltpu.roll(even, half, 1)
        else:
            odd = pltpu.roll(odd, half, 1)
        out_ref[(j // 2) * used : (j // 2 + 1) * used, :] = jnp.where(left, even, odd).astype(bf16)


def project_down(route, slot, arrays, store, offset):
    stored, width, _ = store.shape
    rows = arrays[0][0].shape[1]
    members = sum(value.shape[0] for value, _ in arrays)
    capacity = capacity_of(members, rows // SEG)
    return pl.pallas_call(
        functools.partial(down_kernel, offset, [places for _, places in arrays], capacity),
        out_shape=jax.ShapeDtypeStruct((members // 2 * capacity * SEG, LANES), bf16),
        in_specs=[SMEM, SMEM] + [VMEM] * (len(arrays) + 1),
        out_specs=VMEM,
        scratch_shapes=[
            pltpu.VMEM((stored, members * rows, LANES), f32),
            pltpu.VMEM((members, (capacity + 1) * SEG, LANES), f32),
        ],
        compiler_params=params(12),
        cost_estimate=cost(2 * members * rows * width * stored * LANES, 2e6),
        name="down",
    )(route, slot, *[value for value, _ in arrays], store)


def up_kernel(
    offset, members, capacity, route_ref, slot_ref, rank_ref, store_ref, keep_ref, send_ref, l_scr, y_scr
):
    stored = store_ref.shape[0]
    width = store_ref.shape[1]
    rows = keep_ref.shape[1]
    seg_count = rows // SEG
    half = LANES // 2
    used = capacity * SEG
    table = served(route_ref, slot_ref, members, seg_count, capacity)
    left = lax.broadcasted_iota(jnp.int32, (used, LANES), 1) < half
    l_scr[...] = jnp.zeros_like(l_scr)
    for j in range(members):
        value = rank_ref[(j // 2) * used : (j // 2 + 1) * used, :].astype(f32)
        if (j % 2 == 1) != offset:
            value = pltpu.roll(value, half, 1)
        value = jnp.where(left != offset, value, 0.0)
        y_scr[j * used : (j + 1) * used, :LANES] = value
    for j in range(members):
        for k in range(seg_count):
            index, place = table[j * seg_count + k]
            source = j * used + jnp.minimum(place, capacity - 1) * SEG
            value = y_scr[pl.ds(pl.multiple_of(source, SEG), SEG), :LANES]
            target = j * (used + SEG) + place * SEG
            l_scr[jnp.maximum(index, 0), pl.ds(pl.multiple_of(target, SEG), SEG), :] = value.astype(
                bf16
            )
    lhs = jnp.concatenate(
        [
            jnp.concatenate(
                [l_scr[a, j * (used + SEG) : j * (used + SEG) + used, :] for j in range(members)],
                axis=0,
            )
            for a in range(stored)
        ],
        axis=1,
    )
    piece = min(width, 2 * LANES)
    for n in range(0, width, piece):
        factors = jnp.concatenate(
            [store_ref[a, n : n + piece, LANES:] for a in range(stored)], axis=1
        )
        y_scr[:, n : n + piece] = lax.dot_general(lhs, factors, NT, preferred_element_type=f32)
    for j in range(members):
        out_ref = send_ref if j % 2 else keep_ref
        for k in range(seg_count):
            index, place = table[j * seg_count + k]
            source = j * used + jnp.minimum(place, capacity - 1) * SEG
            value = y_scr[pl.ds(pl.multiple_of(source, SEG), SEG), :]
            out_ref[j // 2, k * SEG : (k + 1) * SEG, :] = jnp.where(index >= 0, value, 0.0).astype(
                bf16
            )


def project_up(route, slot, rank, store, members, rows, offset):
    stored, width, _ = store.shape
    capacity = capacity_of(members, rows // SEG)
    half = jax.ShapeDtypeStruct((members // 2, rows, width), bf16)
    return pl.pallas_call(
        functools.partial(up_kernel, offset, members, capacity),
        out_shape=(half, half),
        in_specs=[SMEM, SMEM, VMEM, VMEM],
        out_specs=(VMEM, VMEM),
        scratch_shapes=[
            pltpu.VMEM((stored, members * (capacity + 1) * SEG, LANES), bf16),
            pltpu.VMEM((members * capacity * SEG, width), f32),
        ],
        compiler_params=params(12),
        cost_estimate=cost(members * rows * width * stored * LANES, 2e6),
        name="up",
    )(route, slot, rank, store)


def assemble_kernel(offsets, *refs):
    inputs, (out_ref, sem) = refs[: len(offsets)], refs[len(offsets) :]
    index = lax.axis_index("tensor")
    copies = []
    for i, (ref, offset) in enumerate(zip(inputs, offsets)):
        width = ref.shape[1]
        start = pl.multiple_of((index ^ offset) * width, LANES)
        copies.append(pltpu.make_async_copy(ref, out_ref.at[:, pl.ds(start, width)], sem.at[i]))
    for copy in copies:
        copy.start()
    for copy in copies:
        copy.wait()


def assemble(blocks):
    rows, width = blocks[0][0].shape
    count = len(blocks)
    return pl.pallas_call(
        functools.partial(assemble_kernel, [offset for _, offset in blocks]),
        out_shape=jax.ShapeDtypeStruct((rows, count * width), bf16),
        in_specs=[VMEM] * count,
        out_specs=ANY,
        scratch_shapes=[pltpu.SemaphoreType.DMA((count,))],
        compiler_params=params(1),
        cost_estimate=cost(0, 4 * rows * count * width),
        name="assemble",
    )(*[value for value, _ in blocks])


def gather_rows(own, axis, size):
    arrays = [(own, [0])]
    for bit in reversed(range(size.bit_length() - 1)):
        more = []
        for value, places in arrays:
            more.append((flip(value, axis, 1 << bit), [j ^ (1 << bit) for j in places]))
        arrays = arrays + more
    return arrays


def return_rows(keep, send, axis, size):
    addends = [keep]
    for bit in range(size.bit_length() - 1):
        addends.append(flip(send, axis, 1 << bit))
        if 2 << bit < size:
            take = [value[1::2] if value.shape[0] > 1 else value for value in addends]
            total = functools.reduce(jnp.add, [value.astype(f32) for value in take])
            send = total.astype(bf16)
            if 4 << bit < size:
                addends = [value[0::2] for value in addends]
    return addends


def reduce_scatter(attended, weights, bits, steps):
    if bits == 3:
        one, two, three = steps
        far, first, third = block_dot(
            [one ^ two ^ three, three ^ one, one ^ two], attended, weights
        )
        far = flip(far, "tensor", one)
        from_three = flip(first, "tensor", three)
        from_one = flip(third, "tensor", one)
        (second,) = block_dot([two ^ three], attended, weights, [far])
        from_two = flip(second, "tensor", two)
        sums = []
        for step, value in ((one, from_three), (two, from_one), (three, from_two)):
            (send,) = block_dot([step], attended, weights, [value])
            sums.append(flip(send, "tensor", step))
        return sums
    offsets, sums = [0], []
    for step in steps:
        offsets = offsets + [j ^ step for j in offsets]
    blocks = dict(zip(offsets, block_dot(offsets, attended, weights)))
    for n, step in enumerate(steps):
        rest = [0]
        for later in steps[n + 1 :]:
            rest = rest + [j ^ later for j in rest]
        send = jnp.stack([blocks[j ^ step] for j in rest])
        received = flip(send, "tensor", step)
        sums.append(received[0])
        for i, j in enumerate(rest[1:]):
            blocks[j] = (blocks[j].astype(f32) + received[i + 1].astype(f32)).astype(bf16)
    return sums


def all_gather(value, bits, steps):
    if bits == 3:
        one, two, three = steps
        at = {0: value}
        for step in steps:
            at[step] = flip(value, "tensor", step)
        for step, source in ((three, one), (one, two), (two, three)):
            at[step ^ source] = flip(at[source], "tensor", step)
        at[one ^ two ^ three] = flip(at[one ^ two], "tensor", three)
        return [(at[j], j) for j in at]
    blocks = [(value, 0)]
    for step in steps:
        received = flip(jnp.stack([value for value, _ in blocks]), "tensor", step)
        blocks = blocks + [(received[i], j ^ step) for i, (_, j) in enumerate(blocks)]
    return blocks


def body(
    hidden,
    norm_gain,
    query_matrix,
    output_weight,
    kv_pages,
    page_order,
    page_counts,
    page_trims,
    adapter_store,
    store_route,
    store_slot,
):
    tensor_size = lax.axis_size("tensor")
    group_size = lax.axis_size("group")
    tensor_index = lax.axis_index("tensor")
    rows, model = hidden.shape
    width = query_matrix.shape[1]
    heads_dev = width // HD
    split_count = tensor_size // KVH
    part_index = tensor_index % split_count
    slots = kv_pages.shape[0]
    half_size = kv_pages.shape[2]

    route = store_route.reshape(-1)
    gain = norm_gain.reshape(1, model)
    own_rows = scale_own(hidden, gain, width)
    row_blocks = gather_rows(own_rows, "group", group_size)
    query, inv, store = project_query(hidden, gain, query_matrix, adapter_store)

    weight_parts = 4
    depth = width // weight_parts
    weights = []
    for p in range(weight_parts):
        weights.append(fetch(output_weight, p * depth, depth))

    lengths = page_counts[0] * (split_count * half_size) - page_trims[0]
    cosine, sine = tables((lengths - 1).astype(f32))
    trims = page_trims * jnp.where(part_index == split_count - 1, 1, 0)
    owner, mask, row = prepare(page_counts, trims, slots, half_size)

    bits = tensor_size.bit_length() - 1
    steps = [1 << k for k in range(bits - 1)] + [3 << (bits - 2)]

    def adapter(blocks, offset):
        rank = project_down(route, store_slot, blocks, store, offset)
        for step in steps:
            received = flip(rank, "tensor", step)
            rank = (rank.astype(f32) + received.astype(f32)).astype(bf16)
        keep, send = project_up(route, store_slot, rank, store, group_size, rows, offset)
        return return_rows(keep, send, "group", group_size)

    deltas = adapter(row_blocks, False)
    attention = functools.partial(
        attend,
        cosine=cosine,
        sine=sine,
        owner=owner,
        mask=mask,
        row=row,
        order=page_order,
        pages=kv_pages,
    )
    if split_count == 1:
        (attended,) = attention(query, inv, deltas, fused=True)
    else:
        delta = functools.reduce(jnp.add, [value[0].astype(f32) for value in deltas])
        wide = ((query + adapter_scale * delta) * inv).reshape(rows, heads_dev, HD)
        wide = wide * cosine[:, None] + jnp.roll(wide, HD // 2, 2) * sine[:, None]
        queries = wide.astype(bf16)
        levels = split_count.bit_length() - 1
        for level in range(levels):
            partner = flip(queries, "tensor", 1 << level)
            upper = part_index // 2**level % 2
            queries = jnp.where(
                upper == 0,
                jnp.concatenate([queries, partner], axis=1),
                jnp.concatenate([partner, queries], axis=1),
            )
        heads = heads_dev * split_count
        numer, top, total = attention(
            queries.reshape(rows, heads * HD).astype(f32), inv, [], fused=False
        )
        numer = numer.reshape(rows, heads, HD)
        top, total = top[:, :heads], total[:, :heads]
        for level in range(levels):
            other, other_top, other_total = flip((numer, top, total), "tensor", 1 << level)
            joint = jnp.maximum(top, other_top)
            own_scale, other_scale = jnp.exp(top - joint), jnp.exp(other_top - joint)
            numer = numer * own_scale[..., None] + other * other_scale[..., None]
            total = total * own_scale + other_total * other_scale
            top = joint
        attended = (
            lax.dynamic_slice_in_dim(
                numer / total[..., None], part_index * heads_dev, heads_dev, 1
            )
            .reshape(rows, width)
            .astype(bf16)
        )

    row_blocks = gather_rows(attended[None], "group", group_size)
    sums = reduce_scatter(attended, weights, bits, steps)
    deltas = adapter(row_blocks, True)
    finished = finish(attended, weights, sums, deltas, hidden)
    return assemble(all_gather(finished, bits, steps))


def solution(mesh):
    in_specs = (
        P("group", None),
        P(),
        P(None, "tensor"),
        P("tensor", None),
        P("group", "tensor", None, None),
        P("group", None),
        P("group", None),
        P("group", None),
        P("group", "tensor", None),
        P(),
        P(),
    )
    out_specs = P("group", None)

    return jax.shard_map(body, mesh=mesh, in_specs=in_specs, out_specs=out_specs, check_vma=False)
```

time: 169 us -> 154 us (0.911)
  the two profiles are of different devices: /device:TPU:0 before, /device:TPU:12 now
where the time goes in v2:
time: 154 us; the launch traced here: 153 us
  waiting for transfers between devices  85.8 us (56%)
  starting transfers between devices  30.2 us (20%)
  Pallas kernels  30 us (19%)
  local copies, waits for them, and re-layouts  6.17 us (4%)
    ppermute x30, waiting for transfers between devices, flip(): lax.ppermute(value, axis, [(i, i ^ bits) for i in range(lax.axis_size(axi...  85.8 us
    ppermute x30, starting transfers between devices, flip(): lax.ppermute(value, axis, [(i, i ^ bits) for i in range(lax.axis_size(axi...  30.2 us
    pallas_call x1, Pallas kernels, attend(): pl.pallas_call(functools.partial(attention_kernel, heads, len(deltas), fu...  9.03 us
    pallas_call x1, Pallas kernels, project_query(): pl.pallas_call(query_kernel, out_shape=(pltpu.VMEM((rows, width), f32), p...  6.7 us
    unnamed x32, local copies, waits for them, and re-layouts  5.43 us
    pallas_call x2, Pallas kernels, project_down(): pl.pallas_call(functools.partial(down_kernel, offset, [places for _, plac...  3.97 us
    pallas_call x2, Pallas kernels, project_up(): pl.pallas_call(functools.partial(up_kernel, offset, members, capacity), o...  3.5 us
  transfers between devices with their start and end apart: 30, of which 22 were waited for; matrix products, arithmetic and copies ran while one was open for 0% of the time, Pallas kernels for 8%

profile of v2, /device:TPU:12, one launch (start us, length us, event | category | flops | bytes accessed | tf_op | source)
XLA Modules:
  0.0 153.3 jit_solution(13800481273098530485)
XLA Ops:
  4.0 6.6 %collective-permute-done.refs_1_ = bf16[1,128,1024]{2,1,0:T(8,128)(2,1)S(1)} collective-permute-done((bf16[1,128,1024]{2,1,0:T(8,128)(2,1)S(1)}, bf16[1,128,1024]{2,1,0:T(8,128)(2,1)S(1)}, u32[]{:S(2)}, u32[]{:S(2)}) %collective-permute-start) | collective-permute-done | bytes 262176 | tf_op jit(solution)/shard_map/ppermute | solution.py:42
  12.1 2.2 %copy-done.5 = bf16[8,1024,256]{2,1,0:T(8,128)(2,1)S(1)} copy-done((bf16[8,1024,256]{2,1,0:T(8,128)(2,1)S(1)}, bf16[8,1024,256]{2,1,0:T(8,128)(2,1)}, u32[]{:S(2)}) %copy-start.5) | copy-done | bytes 4194328
  14.3 6.7 %query.1 = (f32[128,1024]{1,0:T(8,128)S(1)}, f32[128,1]{1,0:T(8,128)S(1)}, bf16[8,1024,256]{2,1,0:T(8,128)(2,1)S(1)}) custom-call(bf16[128,8192]{1,0:T(8,128)(2,1)S(1)} %copy-done.3, bf16[1,8192]{1,0:T(2,128)(2,1)S(1)} %reshape.32.gain_ref, bf16[8192,1024]{1,0:T(8,128)(2,1)} %weight_ref.5, bf16[8,1024,256]{2,1,0:T(8,128)(2,1)S(1)} %copy-done.5), custom_call_target="tpu_custom_call" | custom-call | flops 2147483648 | bytes 23068672 | tf_op jit(solution)/shard_map/query/pallas_call | solution.py:291
  21.1 2.0 %down.2 = bf16[128,128]{1,0:T(8,128)(2,1)S(1)} custom-call(s32[32]{0:T(128)S(1)} %bitcast.9, s32[32]{0:T(128)S(1)} %copy-done.8, bf16[1,128,1024]{2,1,0:T(8,128)(2,1)S(1)} %own.1.refs_0_, bf16[1,128,1024]{2,1,0:T(8,128)(2,1)S(1)} %collective-permute-done.refs_1_, bf16[1,128,1024]{2,1,0:T(8,128)(2,1)S(1)} %collective-permute-done.1.refs_2_, ...), custom_call_target="tpu_custom_call" | custom-call | flops 1073741824 | bytes 2000000 | tf_op jit(solution)/shard_map/down/pallas_call | solution.py:475
  23.7 3.4 %collective-permute-done.3 = bf16[128,128]{1,0:T(8,128)(2,1)S(1)} collective-permute-done((bf16[128,128]{1,0:T(8,128)(2,1)S(1)}, bf16[128,128]{1,0:T(8,128)(2,1)S(1)}, u32[]{:S(2)}, u32[]{:S(2)}) %collective-permute-start.3) | collective-permute-done | bytes 32800 | tf_op jit(solution)/shard_map/ppermute | solution.py:42
  27.6 3.5 %collective-permute-done.4 = bf16[128,128]{1,0:T(8,128)(2,1)S(1)} collective-permute-done((bf16[128,128]{1,0:T(8,128)(2,1)S(1)}, bf16[128,128]{1,0:T(8,128)(2,1)S(1)}, u32[]{:S(2)}, u32[]{:S(2)}) %collective-permute-start.4) | collective-permute-done | bytes 32800 | tf_op jit(solution)/shard_map/ppermute | solution.py:42
  32.7 2.3 %collective-permute-done.5 = bf16[128,128]{1,0:T(8,128)(2,1)S(1)} collective-permute-done((bf16[128,128]{1,0:T(8,128)(2,1)S(1)}, bf16[128,128]{1,0:T(8,128)(2,1)S(1)}, u32[]{:S(2)}, u32[]{:S(2)}) %collective-permute-start.5) | collective-permute-done | bytes 32800 | tf_op jit(solution)/shard_map/ppermute | solution.py:42
  40.9 6.5 %collective-permute-done.7.refs_2_ = bf16[1,128,1024]{2,1,0:T(8,128)(2,1)S(1)} collective-permute-done((bf16[1,128,1024]{2,1,0:T(8,128)(2,1)S(1)}, bf16[1,128,1024]{2,1,0:T(8,128)(2,1)S(1)}, u32[]{:S(2)}, u32[]{:S(2)}) %collective-permute-start.7) | collective-permute-done | bytes 262176 | tf_op jit(solution)/shard_map/ppermute | solution.py:42
  47.3 9.0 %attend.1.rows_ref = bf16[128,1024]{1,0:T(8,128)(2,1)S(1)} custom-call(s32[1,192]{1,0:T(1,128)S(1)} %copy-done.9, f32[128,1024]{1,0:T(8,128)S(1)} %get-tuple-element.18.query_ref, f32[128,1]{1,0:T(8,128)S(1)} %get-tuple-element.19.inv_ref, bf16[2,128,1024]{2,1,0:T(8,128)(2,1)S(1)} %get-tuple-element.21.refs_0_, ...), custom_call_target="tpu_custom_call" | custom-call | flops 400000000 | bytes 8000000 | tf_op jit(solution)/shard_map/attend/pallas_call | solution.py:197
  57.9 6.0 %collective-permute-done.15.refs_1_ = bf16[1,128,1024]{2,1,0:T(8,128)(2,1)S(1)} collective-permute-done((bf16[1,128,1024]{2,1,0:T(8,128)(2,1)S(1)}, bf16[1,128,1024]{2,1,0:T(8,128)(2,1)S(1)}, u32[]{:S(2)}, u32[]{:S(2)}) %collective-permute-start.15) | collective-permute-done | bytes 262176 | tf_op jit(solution)/shard_map/ppermute | solution.py:42
  65.5 2.0 %down.3 = bf16[128,128]{1,0:T(8,128)(2,1)S(1)} custom-call(s32[32]{0:T(128)S(1)} %bitcast.11, s32[32]{0:T(128)S(1)} %copy-done.8, bf16[1,128,1024]{2,1,0:T(8,128)(2,1)S(1)} %bitcast.8, bf16[1,128,1024]{2,1,0:T(8,128)(2,1)S(1)} %collective-permute-done.15.refs_1_, bf16[1,128,1024]{2,1,0:T(8,128)(2,1)S(1)} %collective-permute-done.16.refs_2_, ...), custom_call_target="tpu_custom_call" | custom-call | flops 1073741824 | bytes 2000000 | tf_op jit(solution)/shard_map/down/pallas_call | solution.py:475
  68.0 3.5 %collective-permute-done.18 = bf16[128,128]{1,0:T(8,128)(2,1)S(1)} collective-permute-done((bf16[128,128]{1,0:T(8,128)(2,1)S(1)}, bf16[128,128]{1,0:T(8,128)(2,1)S(1)}, u32[]{:S(2)}, u32[]{:S(2)}) %collective-permute-start.18) | collective-permute-done | bytes 32800 | tf_op jit(solution)/shard_map/ppermute | solution.py:42
  71.5 2.3 %collective-permute-start.19 = (bf16[128,128]{1,0:T(8,128)(2,1)S(1)}, bf16[128,128]{1,0:T(8,128)(2,1)S(1)}, u32[]{:S(2)}, u32[]{:S(2)}) collective-permute-start(bf16[128,128]{1,0:T(8,128)(2,1)S(1)} %add_convert_fusion.4), channel_id=1, source_target_pairs={{0,2},{1,3},{2,0},{3,1},{4,6},{5,7},{6,4},{7,5},{8,10},{9,11},{10,... | collective-permute-start | bytes 98312 | tf_op jit(solution)/shard_map/ppermute | solution.py:42
  75.7 2.8 %collective-permute-start.20 = (bf16[128,128]{1,0:T(8,128)(2,1)S(1)}, bf16[128,128]{1,0:T(8,128)(2,1)S(1)}, u32[]{:S(2)}, u32[]{:S(2)}) collective-permute-start(bf16[128,128]{1,0:T(8,128)(2,1)S(1)} %add_convert_fusion.3), channel_id=1, source_target_pairs={{0,6},{1,7},{2,4},{3,5},{4,2},{5,3},{6,0},{7,1},{8,14},{9,15},{10,... | collective-permute-start | bytes 98312 | tf_op jit(solution)/shard_map/ppermute | solution.py:42
  87.0 3.1 %collective-permute-start.13 = (bf16[128,1024]{1,0:T(8,128)(2,1)S(1)}, bf16[128,1024]{1,0:T(8,128)(2,1)S(1)}, u32[]{:S(2)}, u32[]{:S(2)}) collective-permute-start(bf16[128,1024]{1,0:T(8,128)(2,1)S(1)} %block_dot.8), channel_id=1, source_target_pairs={{0,2},{1,3},{2,0},{3,1},{4,6},{5,7},{6,4},{7,5},{8,10},{9,11},{10,... | collective-permute-start | bytes 786440 | tf_op jit(solution)/shard_map/ppermute | solution.py:42
  92.0 3.0 %collective-permute-start.11 = (bf16[128,1024]{1,0:T(8,128)(2,1)S(1)}, bf16[128,1024]{1,0:T(8,128)(2,1)S(1)}, u32[]{:S(2)}, u32[]{:S(2)}) collective-permute-start(bf16[128,1024]{1,0:T(8,128)(2,1)S(1)} %block_dot.7), channel_id=1, source_target_pairs={{0,2},{1,3},{2,0},{3,1},{4,6},{5,7},{6,4},{7,5},{8,10},{9,11},{10,... | collective-permute-start | bytes 786440 | tf_op jit(solution)/shard_map/ppermute | solution.py:42
  95.0 2.5 %collective-permute-done.8.refs_4_ = bf16[128,1024]{1,0:T(8,128)(2,1)S(1)} collective-permute-done((bf16[128,1024]{1,0:T(8,128)(2,1)S(1)}, bf16[128,1024]{1,0:T(8,128)(2,1)S(1)}, u32[]{:S(2)}, u32[]{:S(2)}) %collective-permute-start.8) | collective-permute-done | bytes 262176 | tf_op jit(solution)/shard_map/ppermute | solution.py:42
  99.1 3.2 %collective-permute-done.13.refs_4_ = bf16[128,1024]{1,0:T(8,128)(2,1)S(1)} collective-permute-done((bf16[128,1024]{1,0:T(8,128)(2,1)S(1)}, bf16[128,1024]{1,0:T(8,128)(2,1)S(1)}, u32[]{:S(2)}, u32[]{:S(2)}) %collective-permute-start.13) | collective-permute-done | bytes 262176 | tf_op jit(solution)/shard_map/ppermute | solution.py:42
  104.5 3.4 %collective-permute-done.11.refs_5_ = bf16[128,1024]{1,0:T(8,128)(2,1)S(1)} collective-permute-done((bf16[128,1024]{1,0:T(8,128)(2,1)S(1)}, bf16[128,1024]{1,0:T(8,128)(2,1)S(1)}, u32[]{:S(2)}, u32[]{:S(2)}) %collective-permute-start.11) | collective-permute-done | bytes 262176 | tf_op jit(solution)/shard_map/ppermute | solution.py:42
  107.9 7.2 %collective-permute-done.14.refs_6_ = bf16[128,1024]{1,0:T(8,128)(2,1)S(1)} collective-permute-done((bf16[128,1024]{1,0:T(8,128)(2,1)S(1)}, bf16[128,1024]{1,0:T(8,128)(2,1)S(1)}, u32[]{:S(2)}, u32[]{:S(2)}) %collective-permute-start.14) | collective-permute-done | bytes 262176 | tf_op jit(solution)/shard_map/ppermute | solution.py:42
  118.1 6.8 %collective-permute-done.24.refs_2_ = bf16[128,1024]{1,0:T(8,128)(2,1)S(1)} collective-permute-done((bf16[128,1024]{1,0:T(8,128)(2,1)S(1)}, bf16[128,1024]{1,0:T(8,128)(2,1)S(1)}, u32[]{:S(2)}, u32[]{:S(2)}) %collective-permute-start.24) | collective-permute-done | bytes 262176 | tf_op jit(solution)/shard_map/ppermute | solution.py:42
  126.9 12.9 %collective-permute-done.25.refs_3_ = bf16[128,1024]{1,0:T(8,128)(2,1)S(1)} collective-permute-done((bf16[128,1024]{1,0:T(8,128)(2,1)S(1)}, bf16[128,1024]{1,0:T(8,128)(2,1)S(1)}, u32[]{:S(2)}, u32[]{:S(2)}) %collective-permute-start.25) | collective-permute-done | bytes 262176 | tf_op jit(solution)/shard_map/ppermute | solution.py:42
  140.8 4.6 %collective-permute-done.26.refs_4_ = bf16[128,1024]{1,0:T(8,128)(2,1)S(1)} collective-permute-done((bf16[128,1024]{1,0:T(8,128)(2,1)S(1)}, bf16[128,1024]{1,0:T(8,128)(2,1)S(1)}, u32[]{:S(2)}, u32[]{:S(2)}) %collective-permute-start.26) | collective-permute-done | bytes 262176 | tf_op jit(solution)/shard_map/ppermute | solution.py:42
  146.1 5.6 %collective-permute-done.29.refs_7_ = bf16[128,1024]{1,0:T(8,128)(2,1)S(1)} collective-permute-done((bf16[128,1024]{1,0:T(8,128)(2,1)S(1)}, bf16[128,1024]{1,0:T(8,128)(2,1)S(1)}, u32[]{:S(2)}, u32[]{:S(2)}) %collective-permute-start.29) | collective-permute-done | bytes 262176 | tf_op jit(solution)/shard_map/ppermute | solution.py:42
  (101 shorter events, 41.8 us)
Async XLA Ops:
  2.4 8.1 %collective-permute-start = (bf16[1,128,1024]{2,1,0:T(8,128)(2,1)S(1)}, bf16[1,128,1024]{2,1,0:T(8,128)(2,1)S(1)}, u32[]{:S(2)}, u32[]{:S(2)}) collective-permute-start(bf16[1,128,1024]{2,1,0:T(8,128)(2,1)S(1)} %own.1.refs_0_), channel_id=1, source_target_pairs={{0,16},{8,24},{16,0},{24,8},{1,17},{9,25},{17,1},{25,9},{2,18},{10... | collective-permute-start | bytes 786440 | tf_op jit(solution)/shard_map/ppermute | solution.py:42
  4.0 17.1 %collective-permute-start.1 = (bf16[1,128,1024]{2,1,0:T(8,128)(2,1)S(1)}, bf16[1,128,1024]{2,1,0:T(8,128)(2,1)S(1)}, u32[]{:S(2)}, u32[]{:S(2)}) collective-permute-start(bf16[1,128,1024]{2,1,0:T(8,128)(2,1)S(1)} %own.1.refs_0_), channel_id=1, source_target_pairs={{0,8},{8,0},{16,24},{24,16},{1,9},{9,1},{17,25},{25,17},{2,10},{10... | collective-permute-start | bytes 786440 | tf_op jit(solution)/shard_map/ppermute | solution.py:42
  10.5 10.5 %collective-permute-start.2 = (bf16[1,128,1024]{2,1,0:T(8,128)(2,1)S(1)}, bf16[1,128,1024]{2,1,0:T(8,128)(2,1)S(1)}, u32[]{:S(2)}, u32[]{:S(2)}) collective-permute-start(bf16[1,128,1024]{2,1,0:T(8,128)(2,1)S(1)} %collective-permute-done.refs_1_), channel_id=1, source_target_pairs={{0,8},{8,0},{16,24},{24,16},{1,9},{9,1},{17,25},{25,17},{2,10},{10... | collective-permute-start | bytes 786440 | tf_op jit(solution)/shard_map/ppermute | solution.py:42
  38.9 8.4 %collective-permute-start.7 = (bf16[1,128,1024]{2,1,0:T(8,128)(2,1)S(1)}, bf16[1,128,1024]{2,1,0:T(8,128)(2,1)S(1)}, u32[]{:S(2)}, u32[]{:S(2)}) collective-permute-start(bf16[1,128,1024]{2,1,0:T(8,128)(2,1)S(1)} %add_convert_fusion.1), channel_id=1, source_target_pairs={{0,16},{8,24},{16,0},{24,8},{1,17},{9,25},{17,1},{25,9},{2,18},{10... | collective-permute-start | bytes 786440 | tf_op jit(solution)/shard_map/ppermute | solution.py:42
  56.4 7.6 %collective-permute-start.15 = (bf16[1,128,1024]{2,1,0:T(8,128)(2,1)S(1)}, bf16[1,128,1024]{2,1,0:T(8,128)(2,1)S(1)}, u32[]{:S(2)}, u32[]{:S(2)}) collective-permute-start(bf16[1,128,1024]{2,1,0:T(8,128)(2,1)S(1)} %bitcast.6), channel_id=1, source_target_pairs={{0,16},{8,24},{16,0},{24,8},{1,17},{9,25},{17,1},{25,9},{2,18},{10... | collective-permute-start | bytes 786440 | tf_op jit(solution)/shard_map/ppermute | solution.py:42
  57.9 6.0 %collective-permute-start.16 = (bf16[1,128,1024]{2,1,0:T(8,128)(2,1)S(1)}, bf16[1,128,1024]{2,1,0:T(8,128)(2,1)S(1)}, u32[]{:S(2)}, u32[]{:S(2)}) collective-permute-start(bf16[1,128,1024]{2,1,0:T(8,128)(2,1)S(1)} %bitcast.7), channel_id=1, source_target_pairs={{0,8},{8,0},{16,24},{24,16},{1,9},{9,1},{17,25},{25,17},{2,10},{10... | collective-permute-start | bytes 786440 | tf_op jit(solution)/shard_map/ppermute | solution.py:42
  71.5 4.2 %collective-permute-start.19 = (bf16[128,128]{1,0:T(8,128)(2,1)S(1)}, bf16[128,128]{1,0:T(8,128)(2,1)S(1)}, u32[]{:S(2)}, u32[]{:S(2)}) collective-permute-start(bf16[128,128]{1,0:T(8,128)(2,1)S(1)} %add_convert_fusion.4), channel_id=1, source_target_pairs={{0,2},{1,3},{2,0},{3,1},{4,6},{5,7},{6,4},{7,5},{8,10},{9,11},{10,... | collective-permute-start | bytes 98312 | tf_op jit(solution)/shard_map/ppermute | solution.py:42
  75.7 4.7 %collective-permute-start.20 = (bf16[128,128]{1,0:T(8,128)(2,1)S(1)}, bf16[128,128]{1,0:T(8,128)(2,1)S(1)}, u32[]{:S(2)}, u32[]{:S(2)}) collective-permute-start(bf16[128,128]{1,0:T(8,128)(2,1)S(1)} %add_convert_fusion.3), channel_id=1, source_target_pairs={{0,6},{1,7},{2,4},{3,5},{4,2},{5,3},{6,0},{7,1},{8,14},{9,15},{10,... | collective-permute-start | bytes 98312 | tf_op jit(solution)/shard_map/ppermute | solution.py:42
  79.5 7.0 %collective-permute-start.12 = (bf16[128,1024]{1,0:T(8,128)(2,1)S(1)}, bf16[128,1024]{1,0:T(8,128)(2,1)S(1)}, u32[]{:S(2)}, u32[]{:S(2)}) collective-permute-start(bf16[128,1024]{1,0:T(8,128)(2,1)S(1)} %get-tuple-element.28), channel_id=1, source_target_pairs={{0,1},{1,0},{2,3},{3,2},{4,5},{5,4},{6,7},{7,6},{8,9},{9,8},{10,11... | collective-permute-start | bytes 786440 | tf_op jit(solution)/shard_map/ppermute | solution.py:42
  82.2 20.7 %collective-permute-start.21 = (bf16[2,128,1024]{2,1,0:T(8,128)(2,1)S(1)}, bf16[2,128,1024]{2,1,0:T(8,128)(2,1)S(1)}, u32[]{:S(2)}, u32[]{:S(2)}) collective-permute-start(bf16[2,128,1024]{2,1,0:T(8,128)(2,1)S(1)} %get-tuple-element.30), channel_id=1, source_target_pairs={{0,8},{8,0},{16,24},{24,16},{1,9},{9,1},{17,25},{25,17},{2,10},{10... | collective-permute-start | bytes 1572872 | tf_op jit(solution)/shard_map/ppermute | solution.py:42
  82.2 9.3 %collective-permute-start.10 = (bf16[128,1024]{1,0:T(8,128)(2,1)S(1)}, bf16[128,1024]{1,0:T(8,128)(2,1)S(1)}, u32[]{:S(2)}, u32[]{:S(2)}) collective-permute-start(bf16[128,1024]{1,0:T(8,128)(2,1)S(1)} %get-tuple-element.27), channel_id=1, source_target_pairs={{0,1},{1,0},{2,3},{3,2},{4,5},{5,4},{6,7},{7,6},{8,9},{9,8},{10,11... | collective-permute-start | bytes 786440 | tf_op jit(solution)/shard_map/ppermute | solution.py:42
  83.5 14.0 %collective-permute-start.8 = (bf16[128,1024]{1,0:T(8,128)(2,1)S(1)}, bf16[128,1024]{1,0:T(8,128)(2,1)S(1)}, u32[]{:S(2)}, u32[]{:S(2)}) collective-permute-start(bf16[128,1024]{1,0:T(8,128)(2,1)S(1)} %get-tuple-element.26), channel_id=1, source_target_pairs={{0,6},{1,7},{2,4},{3,5},{4,2},{5,3},{6,0},{7,1},{8,14},{9,15},{10,... | collective-permute-start | bytes 786440 | tf_op jit(solution)/shard_map/ppermute | solution.py:42
  87.0 15.3 %collective-permute-start.13 = (bf16[128,1024]{1,0:T(8,128)(2,1)S(1)}, bf16[128,1024]{1,0:T(8,128)(2,1)S(1)}, u32[]{:S(2)}, u32[]{:S(2)}) collective-permute-start(bf16[128,1024]{1,0:T(8,128)(2,1)S(1)} %block_dot.8), channel_id=1, source_target_pairs={{0,2},{1,3},{2,0},{3,1},{4,6},{5,7},{6,4},{7,5},{8,10},{9,11},{10,... | collective-permute-start | bytes 786440 | tf_op jit(solution)/shard_map/ppermute | solution.py:42
  92.0 15.9 %collective-permute-start.11 = (bf16[128,1024]{1,0:T(8,128)(2,1)S(1)}, bf16[128,1024]{1,0:T(8,128)(2,1)S(1)}, u32[]{:S(2)}, u32[]{:S(2)}) collective-permute-start(bf16[128,1024]{1,0:T(8,128)(2,1)S(1)} %block_dot.7), channel_id=1, source_target_pairs={{0,2},{1,3},{2,0},{3,1},{4,6},{5,7},{6,4},{7,5},{8,10},{9,11},{10,... | collective-permute-start | bytes 786440 | tf_op jit(solution)/shard_map/ppermute | solution.py:42
  98.0 10.0 %collective-permute-start.9 = (bf16[128,1024]{1,0:T(8,128)(2,1)S(1)}, bf16[128,1024]{1,0:T(8,128)(2,1)S(1)}, u32[]{:S(2)}, u32[]{:S(2)}) collective-permute-start(bf16[128,1024]{1,0:T(8,128)(2,1)S(1)} %block_dot.6), channel_id=1, source_target_pairs={{0,1},{1,0},{2,3},{3,2},{4,5},{5,4},{6,7},{7,6},{8,9},{9,8},{10,11... | collective-permute-start | bytes 786440 | tf_op jit(solution)/shard_map/ppermute | solution.py:42
  102.8 12.4 %collective-permute-start.14 = (bf16[128,1024]{1,0:T(8,128)(2,1)S(1)}, bf16[128,1024]{1,0:T(8,128)(2,1)S(1)}, u32[]{:S(2)}, u32[]{:S(2)}) collective-permute-start(bf16[128,1024]{1,0:T(8,128)(2,1)S(1)} %block_dot.9), channel_id=1, source_target_pairs={{0,6},{1,7},{2,4},{3,5},{4,2},{5,3},{6,0},{7,1},{8,14},{9,15},{10,... | collective-permute-start | bytes 786440 | tf_op jit(solution)/shard_map/ppermute | solution.py:42
  102.9 12.2 %collective-permute-start.22 = (bf16[1,128,1024]{2,1,0:T(8,128)(2,1)S(1)}, bf16[1,128,1024]{2,1,0:T(8,128)(2,1)S(1)}, u32[]{:S(2)}, u32[]{:S(2)}) collective-permute-start(bf16[1,128,1024]{2,1,0:T(8,128)(2,1)S(1)} %add_convert_fusion), channel_id=1, source_target_pairs={{0,16},{8,24},{16,0},{24,8},{1,17},{9,25},{17,1},{25,9},{2,18},{10... | collective-permute-start | bytes 786440 | tf_op jit(solution)/shard_map/ppermute | solution.py:42
  115.9 9.0 %collective-permute-start.24 = (bf16[128,1024]{1,0:T(8,128)(2,1)S(1)}, bf16[128,1024]{1,0:T(8,128)(2,1)S(1)}, u32[]{:S(2)}, u32[]{:S(2)}) collective-permute-start(bf16[128,1024]{1,0:T(8,128)(2,1)S(1)} %finish.1.refs_0_), channel_id=1, source_target_pairs={{0,2},{1,3},{2,0},{3,1},{4,6},{5,7},{6,4},{7,5},{8,10},{9,11},{10,... | collective-permute-start | bytes 786440 | tf_op jit(solution)/shard_map/ppermute | solution.py:42
  116.0 10.7 %collective-permute-start.23 = (bf16[128,1024]{1,0:T(8,128)(2,1)S(1)}, bf16[128,1024]{1,0:T(8,128)(2,1)S(1)}, u32[]{:S(2)}, u32[]{:S(2)}) collective-permute-start(bf16[128,1024]{1,0:T(8,128)(2,1)S(1)} %finish.1.refs_0_), channel_id=1, source_target_pairs={{0,1},{1,0},{2,3},{3,2},{4,5},{5,4},{6,7},{7,6},{8,9},{9,8},{10,11... | collective-permute-start | bytes 786440 | tf_op jit(solution)/shard_map/ppermute | solution.py:42
  117.6 22.2 %collective-permute-start.25 = (bf16[128,1024]{1,0:T(8,128)(2,1)S(1)}, bf16[128,1024]{1,0:T(8,128)(2,1)S(1)}, u32[]{:S(2)}, u32[]{:S(2)}) collective-permute-start(bf16[128,1024]{1,0:T(8,128)(2,1)S(1)} %finish.1.refs_0_), channel_id=1, source_target_pairs={{0,6},{1,7},{2,4},{3,5},{4,2},{5,3},{6,0},{7,1},{8,14},{9,15},{10,... | collective-permute-start | bytes 786440 | tf_op jit(solution)/shard_map/ppermute | solution.py:42
  124.9 14.9 %collective-permute-start.27 = (bf16[128,1024]{1,0:T(8,128)(2,1)S(1)}, bf16[128,1024]{1,0:T(8,128)(2,1)S(1)}, u32[]{:S(2)}, u32[]{:S(2)}) collective-permute-start(bf16[128,1024]{1,0:T(8,128)(2,1)S(1)} %collective-permute-done.24.refs_2_), channel_id=1, source_target_pairs={{0,1},{1,0},{2,3},{3,2},{4,5},{5,4},{6,7},{7,6},{8,9},{9,8},{10,11... | collective-permute-start | bytes 786440 | tf_op jit(solution)/shard_map/ppermute | solution.py:42
  126.7 18.7 %collective-permute-start.26 = (bf16[128,1024]{1,0:T(8,128)(2,1)S(1)}, bf16[128,1024]{1,0:T(8,128)(2,1)S(1)}, u32[]{:S(2)}, u32[]{:S(2)}) collective-permute-start(bf16[128,1024]{1,0:T(8,128)(2,1)S(1)} %collective-permute-done.23.refs_1_), channel_id=1, source_target_pairs={{0,6},{1,7},{2,4},{3,5},{4,2},{5,3},{6,0},{7,1},{8,14},{9,15},{10,... | collective-permute-start | bytes 786440 | tf_op jit(solution)/shard_map/ppermute | solution.py:42
  139.8 6.4 %collective-permute-start.28 = (bf16[128,1024]{1,0:T(8,128)(2,1)S(1)}, bf16[128,1024]{1,0:T(8,128)(2,1)S(1)}, u32[]{:S(2)}, u32[]{:S(2)}) collective-permute-start(bf16[128,1024]{1,0:T(8,128)(2,1)S(1)} %collective-permute-done.25.refs_3_), channel_id=1, source_target_pairs={{0,2},{1,3},{2,0},{3,1},{4,6},{5,7},{6,4},{7,5},{8,10},{9,11},{10,... | collective-permute-start | bytes 786440 | tf_op jit(solution)/shard_map/ppermute | solution.py:42
  139.8 12.0 %collective-permute-start.29 = (bf16[128,1024]{1,0:T(8,128)(2,1)S(1)}, bf16[128,1024]{1,0:T(8,128)(2,1)S(1)}, u32[]{:S(2)}, u32[]{:S(2)}) collective-permute-start(bf16[128,1024]{1,0:T(8,128)(2,1)S(1)} %collective-permute-done.27.refs_5_), channel_id=1, source_target_pairs={{0,6},{1,7},{2,4},{3,5},{4,2},{5,3},{6,0},{7,1},{8,14},{9,15},{10,... | collective-permute-start | bytes 786440 | tf_op jit(solution)/shard_map/ppermute | solution.py:42
  (22 other events, 420.2 us)
